TPU v7x, 1024 devices: a whole 8x8x8 slice. The times are simulated.
1024 devices in a mesh: member: 16 (over y, core), dx: 16 (over x, z_hi), dy: 4 (over z_lo).
Axes of the slice: x: 8, y: 8, z: 8 (z_hi: 2, z_lo: 4; z = z_hi * 4 + z_lo), core: 2. Of those that a mesh axis runs over, the one named last changes fastest.
Arguments:
- perturbed_states: float32 [16, 4, 8, 256, 512], P('member', None, None, 'dx', 'dy'), may hold values from -6 to 6
- control: float32 [16, 4, 8, 256, 512], P('member', None, None, 'dx', 'dy'), may hold values from -6 to 6
- owner: int32 [16], replicated, may hold values from 0 to 15, each once
- map_factor: float32 [256, 512], P('dx', 'dy'), may hold values from 0.5 to 2
- terrain: int32 [256, 512], P('dx', 'dy'), may hold values from 0 to 3
Outputs:
- forecast: float32 [16, 4, 8, 256, 512], P('member', None, None, 'dx', 'dy')
Inputs may be any that keep to these rules, and one draw needn't show every extreme that they name: `owner`: a permutation of the member indices.
All inputs are finite; a program needn't handle non-finite values.
Results may differ from a plain program's by a relative error of at most 0.0003.
Values sent between devices are 32-bit elements; how exact they have to be, the bound alone decides.
A program may use at most 32 MiB of HBM per device.

v0:
```python
import jax
import jax.numpy as jnp
from jax import lax
from jax.sharding import PartitionSpec as P

STEPS = 4


integration_step = 0.2
diffusion = 0.1


def extended(value, sides, width):
    for axis, dim in sides:
        peers, length = (lax.axis_size(axis), value.shape[dim])
        up = [(i, (i + 1) % peers) for i in range(peers - 1)]
        down = [(j, i) for i, j in up]
        last = lax.slice_in_dim(value, length - width, length, axis=dim)
        first = lax.slice_in_dim(value, 0, width, axis=dim)
        before = lax.ppermute(last, axis, up)
        after = lax.ppermute(first, axis, down)
        value = jnp.concatenate([before, value, after], axis=dim)
    return value


def advance(padded, metric, vertical_level_mask):
    middle_point = padded[:, :, 1:-1, 1:-1]
    east = padded[:, :, 2:, 1:-1]
    west = padded[:, :, :-2, 1:-1]
    north = padded[:, :, 1:-1, 2:]
    south = padded[:, :, 1:-1, :-2]
    gradient_along_x = (east - west) * 0.5
    grad_y = (north - south) * 0.5
    stacked = jnp.pad(middle_point, ((0, 0), (1, 1), (0, 0), (0, 0)))
    laplace = east + west + north + south + stacked[:, 2:] + stacked[:, :-2] - 6.0 * middle_point
    wind_x = middle_point[0]
    meridional_velocity = middle_point[1]
    trend = (
        -metric * (wind_x * gradient_along_x + meridional_velocity * grad_y) + diffusion * laplace
    )
    extra = jnp.stack(
        [
            -metric * gradient_along_x[2],
            -metric * grad_y[2],
            -metric * (gradient_along_x[0] + grad_y[1]),
            jnp.zeros_like(wind_x),
        ]
    )
    return vertical_level_mask * (middle_point + integration_step * (trend + extra))


def own_weight(owner, members, here):
    ranks = lax.broadcasted_iota(jnp.int32, (members,), 0)
    per_rank = 2.0 * (members - ranks.astype(jnp.float32)) / (members * (members + 1.0))
    return jnp.sum(jnp.where(owner == here, per_rank, jnp.zeros_like(per_rank)))


def on_device(perturbed_states, control, owner, map_factor, terrain):
    levels_here = perturbed_states.shape[2]
    cols_x = perturbed_states.shape[3]
    column_count_y = perturbed_states.shape[4]
    members = lax.axis_size("member")
    levels = lax.broadcasted_iota(jnp.int32, (levels_here, cols_x, column_count_y), 0)
    vertical_level_mask = (levels >= terrain[None]).astype(jnp.float32)
    weighted = own_weight(owner, members, lax.axis_index("member")) * control[0]
    total, chosen = lax.psum((perturbed_states[0], weighted), "member")
    mean = total / members
    state = chosen + perturbed_states[0] - mean
    for number in range(STEPS):
        padded = extended(state, (("dx", 2), ("dy", 3)), 1)
        state = advance(padded, map_factor, vertical_level_mask)
    return state[None]


def solution(mesh):
    placed = (
        P("member", None, None, "dx", "dy"),
        P("member", None, None, "dx", "dy"),
        P(),
        P("dx", "dy"),
        P("dx", "dy"),
    )
    return jax.shard_map(
        on_device,
        mesh=mesh,
        in_specs=placed,
        out_specs=P("member", None, None, "dx", "dy"),
        check_vma=False,
    )
```

profile of v0, /device:TPU:122, one launch (start us, length us, event | category | flops | bytes accessed | tf_op | source)
XLA Modules:
  0.0 269.6 jit_solution(15933073265024971815)
XLA Ops:
  7.8 2.3 multiply_bitcast_fusion
  10.1 129.2 %all-reduce.7.cloned.1.call-done = (f32[4,8,16,128]{3,2,1,0:T(8,128)}, f32[4,8,16,128]{3,2,1,0:T(8,128)}) async-done(((f32[4,8,16,128]{3,2,1,0:T(8,128)}, f32[4,8,16,128]{3,2,1,0:T(8,128)}), (f32[4,8,16,128]{3,2,1,0:T(8,128)}, f32[4,8,16,128]{3,2,1,0:T(8,128)})) %all-reduce.7.cloned.1.call-update) | async-done | bytes 524304 | tf_op jit(solution)/shard_map/psum | solution.py:66
  140.5 9.6 %collective-permute-start = (f32[4,8,1,128]{3,2,1,0:T(1,128)S(1)}, f32[4,8,1,128]{3,2,1,0:T(1,128)S(1)}, u32[]{:S(2)}, u32[]{:S(2)}) collective-permute-start(f32[4,8,1,128]{3,2,1,0:T(1,128)S(1)} %get-tuple-element.50), channel_id=1, source_target_pairs={{4,0},{8,4},{12,8},{16,12},{20,16},{24,20},{28,24},{32,28},{36,32}... | collective-permute-start | bytes 49160 | tf_op jit(solution)/shard_map/ppermute | solution.py:21
  150.1 1.9 collective-permute-start.1
  152.2 8.4 %collective-permute-done.1 = f32[4,8,1,128]{3,2,1,0:T(1,128)S(1)} collective-permute-done((f32[4,8,1,128]{3,2,1,0:T(1,128)S(1)}, f32[4,8,1,128]{3,2,1,0:T(1,128)S(1)}, u32[]{:S(2)}, u32[]{:S(2)}) %collective-permute-start.1) | collective-permute-done | bytes 16416 | tf_op jit(solution)/shard_map/ppermute | solution.py:20
  162.1 4.6 %collective-permute-start.3 = (f32[4,8,18,1]{3,2,1,0:T(8,128)S(1)}, f32[4,8,18,1]{3,2,1,0:T(8,128)S(1)}, u32[]{:S(2)}, u32[]{:S(2)}) collective-permute-start(f32[4,8,18,1]{3,2,1,0:T(8,128)S(1)} %get-tuple-element.13), channel_id=1, source_target_pairs={{0,1},{1,2},{2,3},{4,5},{5,6},{6,7},{8,9},{9,10},{10,11},{12,13},{... | collective-permute-start | bytes 6920 | tf_op jit(solution)/shard_map/ppermute | solution.py:20
  166.7 7.2 %collective-permute-done.2 = f32[4,8,18,1]{3,2,1,0:T(8,128)S(1)} collective-permute-done((f32[4,8,18,1]{3,2,1,0:T(8,128)S(1)}, f32[4,8,18,1]{3,2,1,0:T(8,128)S(1)}, u32[]{:S(2)}, u32[]{:S(2)}) %collective-permute-start.2) | collective-permute-done | bytes 2336 | tf_op jit(solution)/shard_map/ppermute | solution.py:21
  173.9 1.7 collective-permute-done.3
  176.6 1.9 collective-permute-start.4
  178.5 7.8 %collective-permute-start.5 = (f32[4,8,1,128]{3,2,1,0:T(1,128)S(1)}, f32[4,8,1,128]{3,2,1,0:T(1,128)S(1)}, u32[]{:S(2)}, u32[]{:S(2)}) collective-permute-start(f32[4,8,1,128]{3,2,1,0:T(1,128)S(1)} %get-tuple-element.45), channel_id=1, source_target_pairs={{0,4},{4,8},{8,12},{12,16},{16,20},{20,24},{24,28},{28,32},{32,36}... | collective-permute-start | bytes 49160 | tf_op jit(solution)/shard_map/ppermute | solution.py:20
  186.4 2.9 %collective-permute-done.5 = f32[4,8,1,128]{3,2,1,0:T(1,128)S(1)} collective-permute-done((f32[4,8,1,128]{3,2,1,0:T(1,128)S(1)}, f32[4,8,1,128]{3,2,1,0:T(1,128)S(1)}, u32[]{:S(2)}, u32[]{:S(2)}) %collective-permute-start.5) | collective-permute-done | bytes 16416 | tf_op jit(solution)/shard_map/ppermute | solution.py:20
  190.8 5.1 %collective-permute-start.7 = (f32[4,8,18,1]{3,2,1,0:T(8,128)S(1)}, f32[4,8,18,1]{3,2,1,0:T(8,128)S(1)}, u32[]{:S(2)}, u32[]{:S(2)}) collective-permute-start(f32[4,8,18,1]{3,2,1,0:T(8,128)S(1)} %get-tuple-element.11), channel_id=1, source_target_pairs={{0,1},{1,2},{2,3},{4,5},{5,6},{6,7},{8,9},{9,10},{10,11},{12,13},{... | collective-permute-start | bytes 6920 | tf_op jit(solution)/shard_map/ppermute | solution.py:20
  196.0 6.4 %collective-permute-done.6 = f32[4,8,18,1]{3,2,1,0:T(8,128)S(1)} collective-permute-done((f32[4,8,18,1]{3,2,1,0:T(8,128)S(1)}, f32[4,8,18,1]{3,2,1,0:T(8,128)S(1)}, u32[]{:S(2)}, u32[]{:S(2)}) %collective-permute-start.6) | collective-permute-done | bytes 2336 | tf_op jit(solution)/shard_map/ppermute | solution.py:21
  204.4 7.5 %collective-permute-start.8 = (f32[4,8,1,128]{3,2,1,0:T(1,128)S(1)}, f32[4,8,1,128]{3,2,1,0:T(1,128)S(1)}, u32[]{:S(2)}, u32[]{:S(2)}) collective-permute-start(f32[4,8,1,128]{3,2,1,0:T(1,128)S(1)} %get-tuple-element.42), channel_id=1, source_target_pairs={{4,0},{8,4},{12,8},{16,12},{20,16},{24,20},{28,24},{32,28},{36,32}... | collective-permute-start | bytes 49160 | tf_op jit(solution)/shard_map/ppermute | solution.py:21
  212.0 2.2 collective-permute-start.9
  214.2 8.3 %collective-permute-done.9 = f32[4,8,1,128]{3,2,1,0:T(1,128)S(1)} collective-permute-done((f32[4,8,1,128]{3,2,1,0:T(1,128)S(1)}, f32[4,8,1,128]{3,2,1,0:T(1,128)S(1)}, u32[]{:S(2)}, u32[]{:S(2)}) %collective-permute-start.9) | collective-permute-done | bytes 16416 | tf_op jit(solution)/shard_map/ppermute | solution.py:20
  224.0 5.1 %collective-permute-start.11 = (f32[4,8,18,1]{3,2,1,0:T(8,128)S(1)}, f32[4,8,18,1]{3,2,1,0:T(8,128)S(1)}, u32[]{:S(2)}, u32[]{:S(2)}) collective-permute-start(f32[4,8,18,1]{3,2,1,0:T(8,128)S(1)} %get-tuple-element.9), channel_id=1, source_target_pairs={{0,1},{1,2},{2,3},{4,5},{5,6},{6,7},{8,9},{9,10},{10,11},{12,13},{... | collective-permute-start | bytes 6920 | tf_op jit(solution)/shard_map/ppermute | solution.py:20
  229.2 3.8 %collective-permute-done.10 = f32[4,8,18,1]{3,2,1,0:T(8,128)S(1)} collective-permute-done((f32[4,8,18,1]{3,2,1,0:T(8,128)S(1)}, f32[4,8,18,1]{3,2,1,0:T(8,128)S(1)}, u32[]{:S(2)}, u32[]{:S(2)}) %collective-permute-start.10) | collective-permute-done | bytes 2336 | tf_op jit(solution)/shard_map/ppermute | solution.py:21
  232.9 1.6 collective-permute-done.11
  235.5 3.3 %collective-permute-start.12 = (f32[4,8,1,128]{3,2,1,0:T(1,128)S(1)}, f32[4,8,1,128]{3,2,1,0:T(1,128)S(1)}, u32[]{:S(2)}, u32[]{:S(2)}) collective-permute-start(f32[4,8,1,128]{3,2,1,0:T(1,128)S(1)} %get-tuple-element.38), channel_id=1, source_target_pairs={{4,0},{8,4},{12,8},{16,12},{20,16},{24,20},{28,24},{32,28},{36,32}... | collective-permute-start | bytes 49160 | tf_op jit(solution)/shard_map/ppermute | solution.py:21
  238.8 6.5 %collective-permute-start.13 = (f32[4,8,1,128]{3,2,1,0:T(1,128)S(1)}, f32[4,8,1,128]{3,2,1,0:T(1,128)S(1)}, u32[]{:S(2)}, u32[]{:S(2)}) collective-permute-start(f32[4,8,1,128]{3,2,1,0:T(1,128)S(1)} %get-tuple-element.37), channel_id=1, source_target_pairs={{0,4},{4,8},{8,12},{12,16},{16,20},{20,24},{24,28},{28,32},{32,36}... | collective-permute-start | bytes 49160 | tf_op jit(solution)/shard_map/ppermute | solution.py:20
  245.3 4.0 %collective-permute-done.13 = f32[4,8,1,128]{3,2,1,0:T(1,128)S(1)} collective-permute-done((f32[4,8,1,128]{3,2,1,0:T(1,128)S(1)}, f32[4,8,1,128]{3,2,1,0:T(1,128)S(1)}, u32[]{:S(2)}, u32[]{:S(2)}) %collective-permute-start.13) | collective-permute-done | bytes 16416 | tf_op jit(solution)/shard_map/ppermute | solution.py:20
  250.8 5.1 %collective-permute-start.15 = (f32[4,8,18,1]{3,2,1,0:T(8,128)S(1)}, f32[4,8,18,1]{3,2,1,0:T(8,128)S(1)}, u32[]{:S(2)}, u32[]{:S(2)}) collective-permute-start(f32[4,8,18,1]{3,2,1,0:T(8,128)S(1)} %get-tuple-element.7), channel_id=1, source_target_pairs={{0,1},{1,2},{2,3},{4,5},{5,6},{6,7},{8,9},{9,10},{10,11},{12,13},{... | collective-permute-start | bytes 6920 | tf_op jit(solution)/shard_map/ppermute | solution.py:20
  256.0 3.8 %collective-permute-done.14 = f32[4,8,18,1]{3,2,1,0:T(8,128)S(1)} collective-permute-done((f32[4,8,18,1]{3,2,1,0:T(8,128)S(1)}, f32[4,8,18,1]{3,2,1,0:T(8,128)S(1)}, u32[]{:S(2)}, u32[]{:S(2)}) %collective-permute-start.14) | collective-permute-done | bytes 2336 | tf_op jit(solution)/shard_map/ppermute | solution.py:21
  (53 shorter events, 15.6 us)
Async XLA Ops:
  6.5 132.8 %all-reduce.7.cloned.1.call-start = ((), (), s32[]{:S(2)}) async-start(), calls=%async_computation | async-start | bytes 1048576 | tf_op jit(solution)/shard_map/psum | solution.py:66
  6.5 0.7 copy-start.3
  10.1 129.3 %copy-start = (f32[1,4,8,16,128]{4,3,2,1,0:T(8,128)S(1)}, f32[1,4,8,16,128]{4,3,2,1,0:T(8,128)}, u32[]{:S(2)}) copy-start(f32[1,4,8,16,128]{4,3,2,1,0:T(8,128)} %param.5) | copy-start | bytes 786436
  140.4 11.6 %copy-start.1 = (s32[16,128]{1,0:T(8,128)S(1)}, s32[16,128]{1,0:T(8,128)}, u32[]{:S(2)}) copy-start(s32[16,128]{1,0:T(8,128)} %param.9) | copy-start | bytes 24580
  140.5 11.7 %collective-permute-start = (f32[4,8,1,128]{3,2,1,0:T(1,128)S(1)}, f32[4,8,1,128]{3,2,1,0:T(1,128)S(1)}, u32[]{:S(2)}, u32[]{:S(2)}) collective-permute-start(f32[4,8,1,128]{3,2,1,0:T(1,128)S(1)} %get-tuple-element.50), channel_id=1, source_target_pairs={{4,0},{8,4},{12,8},{16,12},{20,16},{24,20},{28,24},{32,28},{36,32}... | collective-permute-start | bytes 49160 | tf_op jit(solution)/shard_map/ppermute | solution.py:21
  150.1 2.0 copy-start.2
  150.1 10.4 %collective-permute-start.1 = (f32[4,8,1,128]{3,2,1,0:T(1,128)S(1)}, f32[4,8,1,128]{3,2,1,0:T(1,128)S(1)}, u32[]{:S(2)}, u32[]{:S(2)}) collective-permute-start(f32[4,8,1,128]{3,2,1,0:T(1,128)S(1)} %get-tuple-element.49), channel_id=1, source_target_pairs={{0,4},{4,8},{8,12},{12,16},{16,20},{20,24},{24,28},{28,32},{32,36}... | collective-permute-start | bytes 49160 | tf_op jit(solution)/shard_map/ppermute | solution.py:20
  160.8 13.1 %collective-permute-start.2 = (f32[4,8,18,1]{3,2,1,0:T(8,128)S(1)}, f32[4,8,18,1]{3,2,1,0:T(8,128)S(1)}, u32[]{:S(2)}, u32[]{:S(2)}) collective-permute-start(f32[4,8,18,1]{3,2,1,0:T(8,128)S(1)} %get-tuple-element.14), channel_id=1, source_target_pairs={{1,0},{2,1},{3,2},{5,4},{6,5},{7,6},{9,8},{10,9},{11,10},{13,12},{... | collective-permute-start | bytes 6920 | tf_op jit(solution)/shard_map/ppermute | solution.py:21
  162.1 13.6 %collective-permute-start.3 = (f32[4,8,18,1]{3,2,1,0:T(8,128)S(1)}, f32[4,8,18,1]{3,2,1,0:T(8,128)S(1)}, u32[]{:S(2)}, u32[]{:S(2)}) collective-permute-start(f32[4,8,18,1]{3,2,1,0:T(8,128)S(1)} %get-tuple-element.13), channel_id=1, source_target_pairs={{0,1},{1,2},{2,3},{4,5},{5,6},{6,7},{8,9},{9,10},{10,11},{12,13},{... | collective-permute-start | bytes 6920 | tf_op jit(solution)/shard_map/ppermute | solution.py:20
  176.6 9.8 %collective-permute-start.4 = (f32[4,8,1,128]{3,2,1,0:T(1,128)S(1)}, f32[4,8,1,128]{3,2,1,0:T(1,128)S(1)}, u32[]{:S(2)}, u32[]{:S(2)}) collective-permute-start(f32[4,8,1,128]{3,2,1,0:T(1,128)S(1)} %get-tuple-element.46), channel_id=1, source_target_pairs={{4,0},{8,4},{12,8},{16,12},{20,16},{24,20},{28,24},{32,28},{36,32}... | collective-permute-start | bytes 49160 | tf_op jit(solution)/shard_map/ppermute | solution.py:21
  178.5 10.7 %collective-permute-start.5 = (f32[4,8,1,128]{3,2,1,0:T(1,128)S(1)}, f32[4,8,1,128]{3,2,1,0:T(1,128)S(1)}, u32[]{:S(2)}, u32[]{:S(2)}) collective-permute-start(f32[4,8,1,128]{3,2,1,0:T(1,128)S(1)} %get-tuple-element.45), channel_id=1, source_target_pairs={{0,4},{4,8},{8,12},{12,16},{16,20},{20,24},{24,28},{28,32},{32,36}... | collective-permute-start | bytes 49160 | tf_op jit(solution)/shard_map/ppermute | solution.py:20
  189.5 12.8 %collective-permute-start.6 = (f32[4,8,18,1]{3,2,1,0:T(8,128)S(1)}, f32[4,8,18,1]{3,2,1,0:T(8,128)S(1)}, u32[]{:S(2)}, u32[]{:S(2)}) collective-permute-start(f32[4,8,18,1]{3,2,1,0:T(8,128)S(1)} %get-tuple-element.12), channel_id=1, source_target_pairs={{1,0},{2,1},{3,2},{5,4},{6,5},{7,6},{9,8},{10,9},{11,10},{13,12},{... | collective-permute-start | bytes 6920 | tf_op jit(solution)/shard_map/ppermute | solution.py:21
  190.8 12.7 %collective-permute-start.7 = (f32[4,8,18,1]{3,2,1,0:T(8,128)S(1)}, f32[4,8,18,1]{3,2,1,0:T(8,128)S(1)}, u32[]{:S(2)}, u32[]{:S(2)}) collective-permute-start(f32[4,8,18,1]{3,2,1,0:T(8,128)S(1)} %get-tuple-element.11), channel_id=1, source_target_pairs={{0,1},{1,2},{2,3},{4,5},{5,6},{6,7},{8,9},{9,10},{10,11},{12,13},{... | collective-permute-start | bytes 6920 | tf_op jit(solution)/shard_map/ppermute | solution.py:20
  204.4 9.8 %collective-permute-start.8 = (f32[4,8,1,128]{3,2,1,0:T(1,128)S(1)}, f32[4,8,1,128]{3,2,1,0:T(1,128)S(1)}, u32[]{:S(2)}, u32[]{:S(2)}) collective-permute-start(f32[4,8,1,128]{3,2,1,0:T(1,128)S(1)} %get-tuple-element.42), channel_id=1, source_target_pairs={{4,0},{8,4},{12,8},{16,12},{20,16},{24,20},{28,24},{32,28},{36,32}... | collective-permute-start | bytes 49160 | tf_op jit(solution)/shard_map/ppermute | solution.py:21
  212.0 10.5 %collective-permute-start.9 = (f32[4,8,1,128]{3,2,1,0:T(1,128)S(1)}, f32[4,8,1,128]{3,2,1,0:T(1,128)S(1)}, u32[]{:S(2)}, u32[]{:S(2)}) collective-permute-start(f32[4,8,1,128]{3,2,1,0:T(1,128)S(1)} %get-tuple-element.41), channel_id=1, source_target_pairs={{0,4},{4,8},{8,12},{12,16},{16,20},{20,24},{24,28},{28,32},{32,36}... | collective-permute-start | bytes 49160 | tf_op jit(solution)/shard_map/ppermute | solution.py:20
  222.7 10.2 %collective-permute-start.10 = (f32[4,8,18,1]{3,2,1,0:T(8,128)S(1)}, f32[4,8,18,1]{3,2,1,0:T(8,128)S(1)}, u32[]{:S(2)}, u32[]{:S(2)}) collective-permute-start(f32[4,8,18,1]{3,2,1,0:T(8,128)S(1)} %get-tuple-element.10), channel_id=1, source_target_pairs={{1,0},{2,1},{3,2},{5,4},{6,5},{7,6},{9,8},{10,9},{11,10},{13,12},{... | collective-permute-start | bytes 6920 | tf_op jit(solution)/shard_map/ppermute | solution.py:21
  224.0 10.5 %collective-permute-start.11 = (f32[4,8,18,1]{3,2,1,0:T(8,128)S(1)}, f32[4,8,18,1]{3,2,1,0:T(8,128)S(1)}, u32[]{:S(2)}, u32[]{:S(2)}) collective-permute-start(f32[4,8,18,1]{3,2,1,0:T(8,128)S(1)} %get-tuple-element.9), channel_id=1, source_target_pairs={{0,1},{1,2},{2,3},{4,5},{5,6},{6,7},{8,9},{9,10},{10,11},{12,13},{... | collective-permute-start | bytes 6920 | tf_op jit(solution)/shard_map/ppermute | solution.py:20
  235.5 9.8 %collective-permute-start.12 = (f32[4,8,1,128]{3,2,1,0:T(1,128)S(1)}, f32[4,8,1,128]{3,2,1,0:T(1,128)S(1)}, u32[]{:S(2)}, u32[]{:S(2)}) collective-permute-start(f32[4,8,1,128]{3,2,1,0:T(1,128)S(1)} %get-tuple-element.38), channel_id=1, source_target_pairs={{4,0},{8,4},{12,8},{16,12},{20,16},{24,20},{28,24},{32,28},{36,32}... | collective-permute-start | bytes 49160 | tf_op jit(solution)/shard_map/ppermute | solution.py:21
  238.8 10.4 %collective-permute-start.13 = (f32[4,8,1,128]{3,2,1,0:T(1,128)S(1)}, f32[4,8,1,128]{3,2,1,0:T(1,128)S(1)}, u32[]{:S(2)}, u32[]{:S(2)}) collective-permute-start(f32[4,8,1,128]{3,2,1,0:T(1,128)S(1)} %get-tuple-element.37), channel_id=1, source_target_pairs={{0,4},{4,8},{8,12},{12,16},{16,20},{20,24},{24,28},{28,32},{32,36}... | collective-permute-start | bytes 49160 | tf_op jit(solution)/shard_map/ppermute | solution.py:20
  249.5 10.2 %collective-permute-start.14 = (f32[4,8,18,1]{3,2,1,0:T(8,128)S(1)}, f32[4,8,18,1]{3,2,1,0:T(8,128)S(1)}, u32[]{:S(2)}, u32[]{:S(2)}) collective-permute-start(f32[4,8,18,1]{3,2,1,0:T(8,128)S(1)} %get-tuple-element.8), channel_id=1, source_target_pairs={{1,0},{2,1},{3,2},{5,4},{6,5},{7,6},{9,8},{10,9},{11,10},{13,12},{... | collective-permute-start | bytes 6920 | tf_op jit(solution)/shard_map/ppermute | solution.py:21
  250.8 10.4 %collective-permute-start.15 = (f32[4,8,18,1]{3,2,1,0:T(8,128)S(1)}, f32[4,8,18,1]{3,2,1,0:T(8,128)S(1)}, u32[]{:S(2)}, u32[]{:S(2)}) collective-permute-start(f32[4,8,18,1]{3,2,1,0:T(8,128)S(1)} %get-tuple-element.7), channel_id=1, source_target_pairs={{0,1},{1,2},{2,3},{4,5},{5,6},{6,7},{8,9},{9,10},{10,11},{12,13},{... | collective-permute-start | bytes 6920 | tf_op jit(solution)/shard_map/ppermute | solution.py:20
Sparse Core Ops, SparseCore 0:
  10.2 129.0 all-reduce.6
where the time goes:
time: 270 us
  waiting for transfers between devices  180 us (67%)
  starting transfers between devices  65.9 us (24%)
  between operations  13.7 us (5%)
  other arithmetic  8.47 us (3%)
    psum x1, waiting for transfers between devices, on_device(): total, chosen = lax.psum((perturbed_states[0], weighted), 'member')  129 us
    ppermute x8, starting transfers between devices, extended(): before = lax.ppermute(last, axis, up)  38.3 us
    ppermute x8, waiting for transfers between devices, extended(): before = lax.ppermute(last, axis, up)  29.5 us
    ppermute x8, starting transfers between devices, extended(): after = lax.ppermute(first, axis, down)  27.6 us
    ppermute x8, waiting for transfers between devices, extended(): after = lax.ppermute(first, axis, down)  21.1 us
  transfers between devices with their start and end apart: 17, of which 13 were waited for; matrix products, arithmetic and copies ran while one was open for 0% of the time, Pallas kernels for 0%

commit v1 on v0

v1 whole, which is shorter than its diff:
```python
import functools

import jax
import jax.numpy as jnp
from jax import lax
from jax.experimental import pallas as pl
from jax.experimental.pallas import tpu as pltpu
from jax.sharding import PartitionSpec as P

MESH = pl.DeviceIdType.MESH
F32 = jnp.float32

STEPS = 4
FIELDS = 4
LEV = 8
ROWS = 16
COLS = 128
WIDTH = STEPS
TALL = ROWS + 2 * WIDTH
GROUPS = 4
STRIP = TALL // GROUPS
METRIC, MASK = FIELDS, FIELDS + 1
TILE = (LEV, COLS)

integration_step = 0.2
diffusion = 0.1


def stencil(src, dst, b, metric, mask, level):
    mid = [src[b, f] for f in range(FIELDS)]
    east = [src[b + 1, f] for f in range(FIELDS)]
    west = [src[b - 1, f] for f in range(FIELDS)]
    along_x = metric * mid[0]
    along_y = metric * mid[1]
    new, gx, gy = [], [], []
    for f in range(FIELDS):
        north = pltpu.roll(mid[f], COLS - 1, 1)
        south = pltpu.roll(mid[f], 1, 1)
        above = jnp.where(level < LEV - 1, pltpu.roll(mid[f], LEV - 1, 0), 0.0)
        below = jnp.where(level > 0, pltpu.roll(mid[f], 1, 0), 0.0)
        gx.append(east[f] - west[f])
        gy.append(north - south)
        six = (east[f] + west[f]) + (north + south) + (above + below)
        flow = along_x * gx[f] + along_y * gy[f]
        rate = integration_step * diffusion
        new.append((1.0 - 6.0 * rate) * mid[f] + rate * six + flow)
    new[0] = new[0] + metric * gx[2]
    new[1] = new[1] + metric * gy[2]
    new[2] = new[2] + metric * (gx[0] + gy[1])
    for f in range(FIELDS):
        dst[b, f] = mask * new[f]


def kernel(
    members, nx, ny,
    p_hbm, c_hbm, owner_hbm, map_hbm, ter_hbm, out_hbm,
    pv, cv, ov, owner, mv, tv, s0, s1, q, qr, t, rr, dx_rows, mts, mtr, a0, a1, es, er,
    local_sem, dd_s, dd_r, rs_s, rs_r, ag_s, ag_r, fw_s, fw_r, hx_s, hx_r, ha_s, ha_r, hf_s, hf_r,
    ph_s, ph_r, mt_s, mt_r, ed_s, ed_r,
):
    chips = members // 2
    part = (ROWS // 2) // chips
    me = lax.axis_index("member")
    x = lax.axis_index("dx")
    y = lax.axis_index("dy")
    chip = lax.div(me, 2)
    core = lax.rem(me, 2)
    partner = {"member": me + 1 - 2 * core}
    has_w, has_e = x > 0, x < nx - 1
    has_s, has_n = y > 0, y < ny - 1

    def peer(d):
        return lax.rem(chip + d, chips)

    def source(d):
        return lax.rem(chip + chips - d, chips)

    def top(ch):
        return lax.div(2 * ch, chips)

    def own_b(co, ch):
        return WIDTH + ch * part + (1 - co) * (ROWS // 2) * top(ch) + co * WIDTH

    def halo_b(ch):
        return ch * part + (WIDTH + ROWS) - TALL * top(ch)

    def came_from(ch):
        at = x + 1 - 2 * top(ch)
        return jnp.logical_and(at >= 0, at < nx)

    def remote(src, dst, ss, rs, device):
        return pltpu.make_async_remote_copy(
            src_ref=src, dst_ref=dst, send_sem=ss, recv_sem=rs, device_id=device, device_id_type=MESH
        )

    loads = [
        pltpu.make_async_copy(p_hbm, pv, local_sem.at[0]),
        pltpu.make_async_copy(c_hbm, cv, local_sem.at[1]),
        pltpu.make_async_copy(owner_hbm, owner, local_sem.at[2]),
        pltpu.make_async_copy(map_hbm, mv, local_sem.at[3]),
        pltpu.make_async_copy(ter_hbm, tv, local_sem.at[4]),
    ]
    for load in loads:
        load.start()
    barrier = pltpu.get_barrier_semaphore()

    def greet(device):
        pl.semaphore_signal(barrier, inc=1, device_id=device, device_id_type=MESH)

    pl.when(has_w)(lambda: greet({"dx": x - 1}))
    pl.when(has_e)(lambda: greet({"dx": x + 1}))
    for d in range(1, chips):
        greet({"member": 2 * peer(d) + core})
    greet(partner)
    pl.when(has_s)(lambda: greet({"dy": y - 1}))
    pl.when(has_n)(lambda: greet({"dy": y + 1}))

    level = lax.broadcasted_iota(jnp.int32, TILE, 0)
    lane = lax.broadcasted_iota(jnp.int32, TILE, 1)
    level_f = level.astype(F32)
    zero = jnp.zeros(TILE, F32)

    for load in loads:
        load.wait()
    weight = F32(0.0)
    for rank in range(members):
        value = 2.0 * (members - rank) / (members * (members + 1.0))
        weight = weight + jnp.where(owner[rank] == me, F32(value), F32(0.0))

    def first(r, carry):
        for f in range(FIELDS):
            state = pv[pl.ds(f * LEV * ROWS + r, LEV, stride=ROWS), :]
            other = cv[pl.ds(f * LEV * ROWS + r, LEV, stride=ROWS), :]
            s0[r + WIDTH, f] = state
            q[r, f] = weight * other - (1.0 / members) * state
        return carry

    lax.fori_loop(0, ROWS, first, 0, unroll=2)
    for side, start in ((0, 0), (1, ROWS - WIDTH)):
        mts[side, pl.ds(0, WIDTH), :] = mv[pl.ds(start, WIDTH), :]
        mts[side, pl.ds(WIDTH, WIDTH), :] = tv[pl.ds(start, WIDTH), :].astype(F32)

    def empty(b0, side):
        def body():
            for b in range(WIDTH):
                for f in range(FIELDS):
                    s0[b0 + b, f] = zero
                    dx_rows[b0 + b, f] = zero
            mtr[side, pl.ds(0, WIDTH), :] = jnp.ones((WIDTH, COLS), F32)
            mtr[side, pl.ds(WIDTH, WIDTH), :] = jnp.full((WIDTH, COLS), F32(2 * LEV))
        return body

    pl.when(jnp.logical_not(has_w))(empty(0, 1))
    pl.when(jnp.logical_not(has_e))(empty(WIDTH + ROWS, 0))

    def no_edge(side):
        def body():
            for f in range(FIELDS + 2):
                er[side, f] = zero
        return body

    pl.when(jnp.logical_not(has_s))(no_edge(0))
    pl.when(jnp.logical_not(has_n))(no_edge(1))

    pl.semaphore_wait(
        barrier,
        chips + has_w.astype(jnp.int32) + has_e.astype(jnp.int32) + has_s.astype(jnp.int32) + has_n.astype(jnp.int32),
    )

    far_first = sorted(range(1, chips), key=lambda d: -min(d, chips - d))
    near_first = far_first[::-1]
    order = far_first + [0]

    def dd(i):
        ch = peer(order[i])
        return remote(
            q.at[pl.ds(own_b(1 - core, ch) - WIDTH, part)], qr.at[pl.ds(ch * part, part)],
            dd_s.at[i], dd_r.at[i], partner,
        )

    for i in range(chips):
        dd(i).start()

    def p_halo(side):
        src, dst, step = ((WIDTH, WIDTH + ROWS, -1), (ROWS, 0, 1))[side]
        return remote(
            s0.at[pl.ds(src, WIDTH), pl.ds(0, FIELDS)], s0.at[pl.ds(dst, WIDTH), pl.ds(0, FIELDS)],
            ph_s.at[side], ph_r.at[side], {"dx": x + step},
        )

    def mt_halo(side):
        return remote(mts.at[side], mtr.at[side], mt_s.at[side], mt_r.at[side], {"dx": x + (-1, 1)[side]})

    def to_west():
        mt_halo(0).start()
        p_halo(0).start()

    def to_east():
        mt_halo(1).start()
        p_halo(1).start()

    pl.when(has_w)(to_west)
    pl.when(has_e)(to_east)

    def rs(d):
        return remote(
            t.at[pl.ds(peer(d) * part, part)], rr.at[pl.ds((d - 1) * part, part)],
            rs_s.at[d - 1], rs_r.at[d - 1], {"member": 2 * peer(d) + core},
        )

    for i, d in enumerate(order):
        dd(i).wait_recv()
        ch = peer(d)
        for n in range(part):
            for f in range(FIELDS):
                t[ch * part + n, f] = q[own_b(core, ch) - WIDTH + n, f] + qr[ch * part + n, f]
        if d:
            rs(d).start()

    def factors(r, carry):
        s0[r + WIDTH, METRIC] = jnp.broadcast_to(mv[pl.ds(r, 1), :] * (-0.5 * integration_step), TILE)
        ground = jnp.broadcast_to(tv[pl.ds(r, 1), :], TILE)
        s0[r + WIDTH, MASK] = (level >= ground).astype(F32)
        return carry

    lax.fori_loop(0, ROWS, factors, 0)

    total = [[t[chip * part + n, f] for f in range(FIELDS)] for n in range(part)]
    for d in near_first:
        rs(d).wait_recv()
        for n in range(part):
            for f in range(FIELDS):
                total[n][f] = total[n][f] + rr[(d - 1) * part + n, f]
    mine = own_b(core, chip)
    for n in range(part):
        for f in range(FIELDS):
            dx_rows[mine + n, f] = total[n][f]

    here = pl.ds(mine, part)
    halo_here = pl.ds(halo_b(chip), part)
    lead = core == 0
    at = x + 2 * top(chip) - 1
    gives = jnp.logical_and(lead, jnp.logical_and(at >= 0, at < nx))
    takes = jnp.logical_and(lead, came_from(chip))
    hx = remote(dx_rows.at[here], dx_rows.at[halo_here], hx_s, hx_r, {"dx": at})
    pl.when(gives)(hx.start)

    def ag(d):
        return remote(
            dx_rows.at[here], dx_rows.at[here], ag_s.at[d - 1], ag_r.at[d - 1], {"member": 2 * peer(d) + core}
        )

    def ha(d):
        return remote(
            dx_rows.at[halo_here], dx_rows.at[halo_here], ha_s.at[d - 1], ha_r.at[d - 1],
            {"member": 2 * peer(d) + core},
        )

    def fw(d):
        rows = pl.ds(own_b(core, source(d)), part)
        return remote(dx_rows.at[rows], dx_rows.at[rows], fw_s.at[d], fw_r.at[d], partner)

    def hf(d):
        rows = pl.ds(halo_b(source(d)), part)
        return remote(dx_rows.at[rows], dx_rows.at[rows], hf_s.at[d], hf_r.at[d], partner)

    for d in far_first:
        ag(d).start()
    fw(0).start()

    def halo_factors(side, b0):
        for b in range(WIDTH):
            s0[b0 + b, METRIC] = jnp.broadcast_to(mtr[side, pl.ds(b, 1), :] * (-0.5 * integration_step), TILE)
            ground = jnp.broadcast_to(mtr[side, pl.ds(WIDTH + b, 1), :], TILE)
            s0[b0 + b, MASK] = (level_f >= ground).astype(F32)

    pl.when(has_e)(lambda: mt_halo(0).wait_recv())
    pl.when(has_w)(lambda: mt_halo(1).wait_recv())
    halo_factors(0, WIDTH + ROWS)
    halo_factors(1, 0)

    inner = lax.rem(lane, 16)
    block = lax.div(lane, 16)

    def strip_fields(fields):
        def body(i, carry):
            for f in fields:
                packed = zero
                for g in range(GROUPS):
                    row = s0[g * STRIP + i, f]
                    left = jnp.logical_and(block == g, inner >= WIDTH)
                    right = jnp.logical_and(block == GROUPS + g, inner < 16 - WIDTH)
                    packed = jnp.where(left, pltpu.roll(row, 16 * g + WIDTH, 1), packed)
                    packed = jnp.where(right, pltpu.roll(row, 16 * g + 76, 1), packed)
                a0[i + 1, f] = packed
            return carry

        lax.fori_loop(0, STRIP, body, 0)

    strip_fields((METRIC, MASK))

    for d in near_first:
        ag(d).wait_recv()
        fw(d).start()

    def spread_halo():
        hx.wait_recv()
        for d in far_first:
            ha(d).start()
        hf(0).start()

    pl.when(takes)(spread_halo)
    for d in near_first:
        def pass_on(d=d):
            ha(d).wait_recv()
            hf(d).start()

        pl.when(jnp.logical_and(lead, came_from(source(d))))(pass_on)

    for d in [0] + near_first:
        fw(d).wait_recv()
    pl.when(has_w)(lambda: p_halo(0).wait_send())
    pl.when(has_e)(lambda: p_halo(1).wait_send())
    pl.when(has_e)(lambda: p_halo(0).wait_recv())
    pl.when(has_w)(lambda: p_halo(1).wait_recv())
    for d in [0] + near_first:
        pl.when(jnp.logical_and(core == 1, came_from(source(d))))(lambda d=d: hf(d).wait_recv())

    def begin(b, carry):
        for f in range(FIELDS):
            s0[b, f] = s0[b, f] + dx_rows[b, f]
        return carry

    lax.fori_loop(0, TALL, begin, 0, unroll=2)

    strip_fields(range(FIELDS))
    for f in range(FIELDS + 2):
        north, south = zero, zero
        for i in range(STRIP):
            strip = a0[i + 1, f]
            at_lane = (i // 4) * 64 + (i % 4) * 4
            slot = jnp.logical_and(lax.div(lane, 64) == i // 4, lax.div(inner, 4) == i % 4)
            north = jnp.where(slot, pltpu.roll(strip, (at_lane - 72) % COLS, 1), north)
            south = jnp.where(slot, pltpu.roll(strip, (at_lane - 4) % COLS, 1), south)
        es[0, f] = north
        es[1, f] = south

    def edge(side):
        return remote(es.at[side], er.at[side], ed_s.at[side], ed_r.at[side], {"dy": y + (1, -1)[side]})

    pl.when(has_n)(lambda: edge(0).start())
    pl.when(has_s)(lambda: edge(1).start())

    for step in range(STEPS):
        src, dst = (s0, s1) if step % 2 == 0 else (s1, s0)

        def row(b, carry, src=src, dst=dst):
            stencil(src, dst, b, s0[b, METRIC], s0[b, MASK], level)
            return carry

        lax.fori_loop(step + 1, TALL - step - 1, row, 0, unroll=2)

    pl.when(has_s)(lambda: edge(0).wait_recv())
    pl.when(has_n)(lambda: edge(1).wait_recv())
    for i in range(STRIP):
        at_lane = (i // 4) * 64 + (i % 4) * 4
        left = jnp.logical_and(block < GROUPS, inner < WIDTH)
        right = jnp.logical_and(block >= GROUPS, inner >= 16 - WIDTH)
        for f in range(FIELDS + 2):
            strip = a0[i + 1, f]
            strip = jnp.where(left, pltpu.roll(er[0, f], (-at_lane) % COLS, 1), strip)
            strip = jnp.where(right, pltpu.roll(er[1, f], (76 - at_lane) % COLS, 1), strip)
            a0[i + 1, f] = strip
    for step in range(STEPS):
        src, dst = (a0, a1) if step % 2 == 0 else (a1, a0)
        for f in range(FIELDS):
            src[0, f] = pltpu.roll(src[STRIP, f], 16, 1)
            src[STRIP + 1, f] = pltpu.roll(src[1, f], COLS - 16, 1)

        def strip_row(i, carry, src=src, dst=dst):
            stencil(src, dst, i, a0[i, METRIC], a0[i, MASK], level)
            return carry

        lax.fori_loop(1, STRIP + 1, strip_row, 0, unroll=2)

    for g in range(GROUPS):
        def merge(i, carry, g=g):
            for f in range(FIELDS):
                strip = a0[i + 1, f]
                out = s0[g * STRIP + i, f]
                out = jnp.where(lane < WIDTH, pltpu.roll(strip, (-16 * g - WIDTH) % COLS, 1), out)
                out = jnp.where(lane >= COLS - WIDTH, pltpu.roll(strip, (52 - 16 * g) % COLS, 1), out)
                ov[pl.ds(f * LEV * ROWS + g * STRIP + i - WIDTH, LEV, stride=ROWS), :] = out
            return carry

        lax.fori_loop(max(0, WIDTH - g * STRIP), min(STRIP, WIDTH + ROWS - g * STRIP), merge, 0)
    store = pltpu.make_async_copy(ov, out_hbm, local_sem.at[0])
    store.start()

    for i in range(chips):
        dd(i).wait_send()
    for d in far_first:
        rs(d).wait_send()
        ag(d).wait_send()
    pl.when(gives)(hx.wait_send)

    def halo_sent():
        for d in far_first:
            ha(d).wait_send()

    pl.when(takes)(halo_sent)
    for d in range(chips):
        fw(d).wait_send()
        pl.when(jnp.logical_and(lead, came_from(source(d))))(lambda d=d: hf(d).wait_send())
    pl.when(has_w)(lambda: mt_halo(0).wait_send())
    pl.when(has_e)(lambda: mt_halo(1).wait_send())
    pl.when(has_n)(lambda: edge(0).wait_send())
    pl.when(has_s)(lambda: edge(1).wait_send())
    store.wait()


def solution(mesh):
    members, nx, ny = (mesh.shape[axis] for axis in ("member", "dx", "dy"))
    chips = members // 2
    part = (ROWS // 2) // chips
    flat = FIELDS * LEV * ROWS

    def on_device(states, control, owner, map_factor, terrain):
        any_space = pl.BlockSpec(memory_space=pl.ANY)
        dma = pltpu.SemaphoreType.DMA
        out = pl.pallas_call(
            functools.partial(kernel, members, nx, ny),
            out_shape=jax.ShapeDtypeStruct((flat, COLS), F32),
            in_specs=[any_space] * 5,
            out_specs=any_space,
            scratch_shapes=[
                pltpu.VMEM((flat, COLS), F32),
                pltpu.VMEM((flat, COLS), F32),
                pltpu.VMEM((flat, COLS), F32),
                pltpu.SMEM((members,), jnp.int32),
                pltpu.VMEM((ROWS, COLS), F32),
                pltpu.VMEM((ROWS, COLS), jnp.int32),
                pltpu.VMEM((TALL, FIELDS + 2) + TILE, F32),
                pltpu.VMEM((TALL, FIELDS) + TILE, F32),
                pltpu.VMEM((ROWS, FIELDS) + TILE, F32),
                pltpu.VMEM((ROWS // 2, FIELDS) + TILE, F32),
                pltpu.VMEM((ROWS // 2, FIELDS) + TILE, F32),
                pltpu.VMEM((part * max(chips - 1, 1), FIELDS) + TILE, F32),
                pltpu.VMEM((TALL, FIELDS) + TILE, F32),
                pltpu.VMEM((2,) + TILE, F32),
                pltpu.VMEM((2,) + TILE, F32),
                pltpu.VMEM((STRIP + 2, FIELDS + 2) + TILE, F32),
                pltpu.VMEM((STRIP + 2, FIELDS) + TILE, F32),
                pltpu.VMEM((2, FIELDS + 2) + TILE, F32),
                pltpu.VMEM((2, FIELDS + 2) + TILE, F32),
                dma((5,)),
                dma((chips,)), dma((chips,)),
                dma((chips - 1,)), dma((chips - 1,)),
                dma((chips - 1,)), dma((chips - 1,)),
                dma((chips,)), dma((chips,)),
                dma, dma,
                dma((chips - 1,)), dma((chips - 1,)),
                dma((chips,)), dma((chips,)),
                dma((2,)), dma((2,)),
                dma((2,)), dma((2,)),
                dma((2,)), dma((2,)),
            ],
            compiler_params=pltpu.CompilerParams(collective_id=0, has_side_effects=True),
        )(states.reshape(flat, COLS), control.reshape(flat, COLS), owner, map_factor, terrain)
        return out.reshape(states.shape)

    spread = P("member", None, None, "dx", "dy")
    return jax.shard_map(
        on_device,
        mesh=mesh,
        in_specs=(spread, spread, P(), P("dx", "dy"), P("dx", "dy")),
        out_specs=spread,
        check_vma=False,
    )
```

time: 270 us -> 45.8 us (0.17)
  the two profiles are of different devices: /device:TPU:122 before, /device:TPU:15 now
where the time goes in v1:
time: 45.8 us; the launch traced here: 45.6 us
  Pallas kernels  43.9 us (96%)
  local copies, waits for them, and re-layouts  1.67 us (4%)
    pallas_call x1, Pallas kernels, on_device(): pl.pallas_call(functools.partial(kernel, members, nx, ny), out_shape=jax....  43.9 us
    unnamed x1, local copies, waits for them, and re-layouts  1.67 us

profile of v1, /device:TPU:15, one launch (start us, length us, event | category | flops | bytes accessed | tf_op | source)
XLA Modules:
  0.0 45.6 jit_solution(12545153583482369629)
XLA Ops:
  0.0 43.9 %shard_map.55 = f32[512,128]{1,0:T(8,128)} custom-call(f32[512,128]{1,0:T(8,128)} %bitcast.4, f32[512,128]{1,0:T(8,128)} %bitcast.5, s32[16]{0:T(128)} %owner_hbm.1, f32[16,128]{1,0:T(8,128)} %map_hbm.1, s32[16,128]{1,0:T(8,128)} %ter_hbm.1), custom_call_target="tpu_custom_call" | custom-call | tf_op jit(solution)/shard_map/pallas_call | solution.py:431
  43.9 1.7 %copy.7 = f32[1,4,8,16,128]{4,3,2,1,0:T(8,128)} copy(f32[1,4,8,16,128]{4,3,2,1,0:T(8,128)} %bitcast.3) | data formatting | bytes 524288

commit v2 on v1

v2 whole, which is shorter than its diff:
```python
import functools

import jax
import jax.numpy as jnp
from jax import lax
from jax.experimental import pallas as pl
from jax.experimental.pallas import tpu as pltpu
from jax.sharding import PartitionSpec as P

MESH = pl.DeviceIdType.MESH
F32 = jnp.float32

STEPS = 4
FIELDS = 4
HALF = FIELDS // 2
LEV = 8
ROWS = 16
COLS = 128
WIDTH = STEPS
TALL = ROWS + 2 * WIDTH
GROUPS = 4
STRIP = TALL // GROUPS
METRIC, MASK = FIELDS, FIELDS + 1
TILE = (LEV, COLS)

integration_step = 0.2
diffusion = 0.1


def stencil(src, dst, b, metric, mask, level):
    mid = [src[b, f] for f in range(FIELDS)]
    east = [src[b + 1, f] for f in range(FIELDS)]
    west = [src[b - 1, f] for f in range(FIELDS)]
    along_x = metric * mid[0]
    along_y = metric * mid[1]
    new, gx, gy = [], [], []
    for f in range(FIELDS):
        north = pltpu.roll(mid[f], COLS - 1, 1)
        south = pltpu.roll(mid[f], 1, 1)
        above = jnp.where(level < LEV - 1, pltpu.roll(mid[f], LEV - 1, 0), 0.0)
        below = jnp.where(level > 0, pltpu.roll(mid[f], 1, 0), 0.0)
        gx.append(east[f] - west[f])
        gy.append(north - south)
        six = (east[f] + west[f]) + (north + south) + (above + below)
        flow = along_x * gx[f] + along_y * gy[f]
        rate = integration_step * diffusion
        new.append((1.0 - 6.0 * rate) * mid[f] + rate * six + flow)
    new[0] = new[0] + metric * gx[2]
    new[1] = new[1] + metric * gy[2]
    new[2] = new[2] + metric * (gx[0] + gy[1])
    for f in range(FIELDS):
        dst[b, f] = mask * new[f]


def kernel(
    members, nx, ny,
    p_hbm, c_hbm, owner_hbm, map_hbm, ter_hbm, out,
    pv, cv, owner, mv, tv, s0, s1, s2, s3, s4, q, qr, t, rr, dx_rows, mts, mtr, a0, a1, es, er, hs, hr,
    local_sem, out_s, dd_r, dm_r, rs_r, ag_r, fw_r, hx_s, hx_r, ha_s, ha_r, hf_s, hf_r,
    ph_s, ph_r, mt_s, mt_r, ed_s, ed_r,
):
    chips = members // 2
    part = (ROWS // 2) // chips
    me = lax.axis_index("member")
    x = lax.axis_index("dx")
    y = lax.axis_index("dy")
    chip = lax.div(me, 2)
    core = lax.rem(me, 2)
    partner = {"member": me + 1 - 2 * core}
    has_w, has_e = x > 0, x < nx - 1
    has_s, has_n = y > 0, y < ny - 1
    far_first = sorted(range(1, chips), key=lambda d: -min(d, chips - d))
    near_first = far_first[::-1]
    order = far_first + [0]
    mine = pl.ds(HALF * core, HALF)
    theirs = pl.ds(HALF * (1 - core), HALF)
    sent = []
    pieces = 2 * chips + 2 * (chips - 1) + 2 * (chips - 1) + 2 * chips

    def peer(d):
        return lax.rem(chip + d, chips)

    def source(d):
        return lax.rem(chip + chips - d, chips)

    def top(ch):
        return lax.div(2 * ch, chips)

    def own_b(kind, ch):
        if kind == 0:
            return WIDTH + ch * part + (ROWS // 2) * top(ch)
        return 2 * WIDTH + ch * part

    def halo_b(ch):
        return ch * part + (WIDTH + ROWS) - TALL * top(ch)

    def came_from(ch):
        at = x + 1 - 2 * top(ch)
        return jnp.logical_and(at >= 0, at < nx)

    def remote(src, dst, ss, rs, device):
        return pltpu.make_async_remote_copy(
            src_ref=src, dst_ref=dst, send_sem=ss, recv_sem=rs, device_id=device, device_id_type=MESH
        )

    def arrived(ref, sem):
        pltpu.make_async_copy(ref, ref, sem).wait()

    def same_core(d):
        return {"member": 2 * peer(d) + core}

    loads = [
        pltpu.make_async_copy(p_hbm, pv, local_sem.at[0]),
        pltpu.make_async_copy(c_hbm, cv, local_sem.at[1]),
        pltpu.make_async_copy(owner_hbm, owner, local_sem.at[2]),
        pltpu.make_async_copy(map_hbm, mv, local_sem.at[3]),
        pltpu.make_async_copy(ter_hbm, tv, local_sem.at[4]),
    ]
    for load in loads:
        load.start()
    barrier = pltpu.get_barrier_semaphore()

    def greet(device):
        pl.semaphore_signal(barrier, inc=1, device_id=device, device_id_type=MESH)

    pl.when(has_w)(lambda: greet({"dx": x - 1}))
    pl.when(has_e)(lambda: greet({"dx": x + 1}))
    for d in far_first:
        greet(same_core(d))
    greet(partner)
    pl.when(has_s)(lambda: greet({"dy": y - 1}))
    pl.when(has_n)(lambda: greet({"dy": y + 1}))

    level = lax.broadcasted_iota(jnp.int32, TILE, 0)
    lane = lax.broadcasted_iota(jnp.int32, TILE, 1)
    level_f = level.astype(F32)
    zero = jnp.zeros(TILE, F32)

    for load in loads:
        load.wait()
    weight = F32(0.0)
    for rank in range(members):
        value = 2.0 * (members - rank) / (members * (members + 1.0))
        weight = weight + jnp.where(owner[rank] == me, F32(value), F32(0.0))

    def first(r, carry):
        for f in range(FIELDS):
            state = pv[pl.ds(f * LEV * ROWS + r, LEV, stride=ROWS), :]
            other = cv[pl.ds(f * LEV * ROWS + r, LEV, stride=ROWS), :]
            s0[r + WIDTH, f] = state
            q[r, f] = weight * other - (1.0 / members) * state
        return carry

    lax.fori_loop(0, WIDTH, first, 0, unroll=2)
    lax.fori_loop(ROWS - WIDTH, ROWS, first, 0, unroll=2)
    pl.semaphore_wait(
        barrier,
        chips + has_w.astype(jnp.int32) + has_e.astype(jnp.int32) + has_s.astype(jnp.int32) + has_n.astype(jnp.int32),
    )

    def dd(kind, d):
        rows = pl.ds(own_b(kind, peer(d)) - WIDTH, part)
        return remote(q.at[rows, theirs], qr.at[rows], out_s, dd_r.at[d] if kind == 0 else dm_r, partner)

    def p_halo(side):
        src, dst, step = ((WIDTH, WIDTH + ROWS, -1), (ROWS, 0, 1))[side]
        return remote(
            s0.at[pl.ds(src, WIDTH), pl.ds(0, FIELDS)], s0.at[pl.ds(dst, WIDTH), pl.ds(0, FIELDS)],
            ph_s.at[side], ph_r.at[side], {"dx": x + step},
        )

    def mt_halo(side):
        return remote(mts.at[side], mtr.at[side], mt_s.at[side], mt_r.at[side], {"dx": x + (-1, 1)[side]})

    def rs(kind, d):
        return remote(
            t.at[pl.ds(own_b(kind, peer(d)) - WIDTH, part)], rr.at[kind, pl.ds((d - 1) * part, part)],
            out_s, rs_r.at[kind], same_core(d),
        )

    def swap_and_send(kind):
        if kind == 1:
            arrived(qr.at[pl.ds(WIDTH, ROWS // 2)], dm_r)
        for d in order:
            if kind == 0:
                dd(kind, d).wait_recv()
            b = own_b(kind, peer(d)) - WIDTH
            for n in range(part):
                for f in range(HALF):
                    t[b + n, f] = q[b + n, HALF * core + f] + qr[b + n, f]
            if d:
                rs(kind, d).start()

    for d in order:
        dd(0, d).start()
    pl.when(has_w)(lambda: p_halo(0).start())
    pl.when(has_e)(lambda: p_halo(1).start())
    lax.fori_loop(WIDTH, ROWS - WIDTH, first, 0, unroll=2)
    for d in order:
        dd(1, d).start()
    swap_and_send(0)
    swap_and_send(1)

    for side, start in ((0, 0), (1, ROWS - WIDTH)):
        mts[side, pl.ds(0, WIDTH), :] = mv[pl.ds(start, WIDTH), :]
        mts[side, pl.ds(WIDTH, WIDTH), :] = tv[pl.ds(start, WIDTH), :].astype(F32)
    for side, there in ((0, has_w), (1, has_e)):
        pl.when(there)(lambda side=side: mt_halo(side).start())
        sent.append(lambda side=side, there=there: pl.when(there)(mt_halo(side).wait_send))

    def factors(r, carry):
        s0[r + WIDTH, METRIC] = jnp.broadcast_to(mv[pl.ds(r, 1), :] * (-0.5 * integration_step), TILE)
        ground = jnp.broadcast_to(tv[pl.ds(r, 1), :], TILE)
        s0[r + WIDTH, MASK] = (level >= ground).astype(F32)
        return carry

    lax.fori_loop(0, ROWS, factors, 0)

    def empty(b0, side):
        def body():
            for b in range(WIDTH):
                for f in range(FIELDS):
                    s0[b0 + b, f] = zero
                    dx_rows[b0 + b, f] = zero
            mtr[side, pl.ds(0, WIDTH), :] = jnp.ones((WIDTH, COLS), F32)
            mtr[side, pl.ds(WIDTH, WIDTH), :] = jnp.full((WIDTH, COLS), F32(2 * LEV))
        return body

    pl.when(jnp.logical_not(has_w))(empty(0, 1))
    pl.when(jnp.logical_not(has_e))(empty(WIDTH + ROWS, 0))

    def no_edge(side):
        def body():
            for f in range(FIELDS + 2):
                er[side, f] = zero
            hr[side] = zero
        return body

    pl.when(jnp.logical_not(has_s))(no_edge(0))
    pl.when(jnp.logical_not(has_n))(no_edge(1))

    at = x + 2 * top(chip) - 1
    gives = jnp.logical_and(at >= 0, at < nx)
    takes = came_from(chip)
    halo_here = pl.ds(halo_b(chip), part)
    hx = remote(
        dx_rows.at[pl.ds(own_b(0, chip), part), mine], dx_rows.at[halo_here, mine], hx_s, hx_r, {"dx": at}
    )

    def ag(kind, d):
        rows = pl.ds(own_b(kind, chip), part)
        return remote(
            dx_rows.at[rows, mine], dx_rows.at[rows, mine], out_s, ag_r.at[d - 1], same_core(d)
        )

    def fw(kind, d):
        rows = pl.ds(own_b(kind, source(d)), part)
        return remote(dx_rows.at[rows, mine], dx_rows.at[rows, mine], out_s, fw_r, partner)

    def ha(d):
        return remote(
            dx_rows.at[halo_here, mine], dx_rows.at[halo_here, mine], ha_s, ha_r.at[d - 1], same_core(d)
        )

    def hf(d):
        rows = pl.ds(halo_b(source(d)), part)
        return remote(dx_rows.at[rows, mine], dx_rows.at[rows, mine], hf_s.at[top(source(d))], hf_r.at[top(source(d))], partner)

    for kind in range(2):
        b = own_b(kind, chip)
        total = [[t[b - WIDTH + n, f] for f in range(HALF)] for n in range(part)]
        arrived(rr.at[kind], rs_r.at[kind])
        for d in near_first:
            for n in range(part):
                for f in range(HALF):
                    total[n][f] = total[n][f] + rr[kind, (d - 1) * part + n, f]
        for n in range(part):
            for f in range(HALF):
                dx_rows[b + n, HALF * core + f] = total[n][f]
        if kind == 0:
            pl.when(gives)(hx.start)
            sent.append(lambda: pl.when(gives)(hx.wait_send))
        for d in far_first:
            ag(kind, d).start()
        fw(kind, 0).start()

    def gather(ds):
        for d in ds:
            arrived(dx_rows.at[pl.ds(0, 2 * part), mine], ag_r.at[d - 1])
            for kind in range(2):
                fw(kind, d).start()

    gather(near_first[: chips // 2])
    def spread_halo():
        hx.wait_recv()
        for d in far_first:
            ha(d).start()
        hf(0).start()

    pl.when(takes)(spread_halo)

    sent.append(lambda: pl.when(takes)(lambda: arrived(rr.at[0], ha_s)))
    gather(near_first[chips // 2 :])
    arrived(dx_rows.at[pl.ds(0, ROWS), mine], fw_r)

    pl.when(has_w)(lambda: p_halo(0).wait_send())
    pl.when(has_e)(lambda: p_halo(1).wait_send())

    def begin(b, carry):
        for f in range(FIELDS):
            s0[b, f] = s0[b, f] + dx_rows[b, f]
        return carry

    lax.fori_loop(WIDTH, WIDTH + ROWS, begin, 0, unroll=2)
    states = (s0, s1, s2, s3, s4)
    for step in range(1, STEPS + 1):
        def row(b, carry, src=states[step - 1], dst=states[step]):
            stencil(src, dst, b, s0[b, METRIC], s0[b, MASK], level)
            return carry

        lax.fori_loop(WIDTH + step, WIDTH + ROWS - step, row, 0, unroll=True)

    inner = lax.rem(lane, 16)
    block = lax.div(lane, 16)

    def pack_rows(rows, old):
        def body(f, carry):
            for i in range(STRIP):
                groups = [g for g in range(GROUPS) if g * STRIP + i in rows]
                if not groups:
                    continue
                packed = a0[i + 1, f] if old else zero
                for g in groups:
                    row = s0[g * STRIP + i, f]
                    left = jnp.logical_and(block == g, inner >= WIDTH)
                    right = jnp.logical_and(block == GROUPS + g, inner < 16 - WIDTH)
                    packed = jnp.where(left, pltpu.roll(row, 16 * g + WIDTH, 1), packed)
                    packed = jnp.where(right, pltpu.roll(row, 16 * g + 76, 1), packed)
                a0[i + 1, f] = packed
            return carry
        return body

    inside = range(WIDTH, WIDTH + ROWS)
    outside = [b for b in range(TALL) if b not in inside]
    lax.fori_loop(0, FIELDS + 2, pack_rows(inside, False), 0)

    def halo_factors(side, b0):
        for b in range(WIDTH):
            s0[b0 + b, METRIC] = jnp.broadcast_to(mtr[side, pl.ds(b, 1), :] * (-0.5 * integration_step), TILE)
            ground = jnp.broadcast_to(mtr[side, pl.ds(WIDTH + b, 1), :], TILE)
            s0[b0 + b, MASK] = (level_f >= ground).astype(F32)

    pl.when(has_e)(lambda: mt_halo(0).wait_recv())
    pl.when(has_w)(lambda: mt_halo(1).wait_recv())
    halo_factors(0, WIDTH + ROWS)
    halo_factors(1, 0)
    lax.fori_loop(FIELDS, FIELDS + 2, pack_rows(outside, True), 0)

    for f in range(FIELDS + 2):
        north, south = zero, zero
        for i in range(STRIP):
            strip = a0[i + 1, f]
            at_lane = (i // 4) * 64 + (i % 4) * 4
            slot = jnp.logical_and(lax.div(lane, 64) == i // 4, lax.div(inner, 4) == i % 4)
            north = jnp.where(slot, pltpu.roll(strip, (at_lane - 72) % COLS, 1), north)
            south = jnp.where(slot, pltpu.roll(strip, (at_lane - 4) % COLS, 1), south)
        es[0, f] = north
        es[1, f] = south

    def edge(side):
        return remote(es.at[side], er.at[side], ed_s.at[side], ed_r.at[side], {"dy": y + (1, -1)[side]})

    for side, there in ((0, has_n), (1, has_s)):
        pl.when(there)(lambda side=side: edge(side).start())
        sent.append(lambda side=side, there=there: pl.when(there)(edge(side).wait_send))

    for d in near_first:
        def pass_on(d=d):
            ha(d).wait_recv()
            hf(d).start()

        pl.when(came_from(source(d)))(pass_on)
    pl.when(has_s)(lambda: edge(0).wait_recv())
    pl.when(has_n)(lambda: edge(1).wait_recv())
    for i in range(STRIP):
        at_lane = (i // 4) * 64 + (i % 4) * 4
        left = jnp.logical_and(block < GROUPS, inner < WIDTH)
        right = jnp.logical_and(block >= GROUPS, inner >= 16 - WIDTH)
        for f in range(FIELDS + 2):
            strip = a0[i + 1, f]
            strip = jnp.where(left, pltpu.roll(er[0, f], (-at_lane) % COLS, 1), strip)
            strip = jnp.where(right, pltpu.roll(er[1, f], (76 - at_lane) % COLS, 1), strip)
            a0[i + 1, f] = strip
    for side, there in ((0, has_e), (1, has_w)):
        rows = dx_rows.at[pl.ds(0, WIDTH), mine]
        pl.when(there)(lambda side=side, rows=rows: arrived(rows, hf_r.at[side]))
        sent.append(lambda side=side, there=there, rows=rows: pl.when(there)(lambda: arrived(rows, hf_s.at[side])))
    pl.when(has_e)(lambda: p_halo(0).wait_recv())
    pl.when(has_w)(lambda: p_halo(1).wait_recv())
    lax.fori_loop(0, WIDTH, begin, 0, unroll=2)
    lax.fori_loop(WIDTH + ROWS, TALL, begin, 0, unroll=2)

    lax.fori_loop(0, FIELDS, pack_rows(outside, True), 0)
    north, south = zero, zero
    for f in range(FIELDS):
        for n, b in enumerate(outside):
            at_lane = f * 32 + n * WIDTH
            slot = lax.div(lane, WIDTH) == at_lane // WIDTH
            row = s0[b, f]
            north = jnp.where(slot, pltpu.roll(row, (at_lane + WIDTH) % COLS, 1), north)
            south = jnp.where(slot, pltpu.roll(row, at_lane, 1), south)
    hs[0] = north
    hs[1] = south

    def corner(side):
        return remote(hs.at[side], hr.at[side], ed_s.at[2 + side], ed_r.at[2 + side], {"dy": y + (1, -1)[side]})

    for side, there in ((0, has_n), (1, has_s)):
        pl.when(there)(lambda side=side: corner(side).start())
        sent.append(lambda side=side, there=there: pl.when(there)(corner(side).wait_send))

    for step in range(1, STEPS + 1):
        def rows(j, carry, src=states[step - 1], dst=states[step], step=step):
            for b in (step + j, WIDTH + ROWS - step + j):
                stencil(src, dst, b, s0[b, METRIC], s0[b, MASK], level)
            return carry

        lax.fori_loop(0, WIDTH, rows, 0, unroll=True)

    pl.when(has_s)(lambda: corner(0).wait_recv())
    pl.when(has_n)(lambda: corner(1).wait_recv())
    from_south, from_north = hr[0], hr[1]
    for n, b in enumerate(outside):
        g, i = divmod(b, STRIP)
        left = jnp.logical_and(block == g, inner < WIDTH)
        right = jnp.logical_and(block == GROUPS + g, inner >= 16 - WIDTH)
        for f in range(FIELDS):
            at_lane = f * 32 + n * WIDTH
            strip = a0[i + 1, f]
            strip = jnp.where(left, pltpu.roll(from_south, (16 * g - at_lane) % COLS, 1), strip)
            strip = jnp.where(right, pltpu.roll(from_north, (76 + 16 * g - at_lane) % COLS, 1), strip)
            a0[i + 1, f] = strip
    for step in range(STEPS):
        src, dst = (a0, a1) if step % 2 == 0 else (a1, a0)
        for f in range(FIELDS):
            src[0, f] = pltpu.roll(src[STRIP, f], 16, 1)
            src[STRIP + 1, f] = pltpu.roll(src[1, f], COLS - 16, 1)

        def strip_row(i, carry, src=src, dst=dst):
            stencil(src, dst, i, a0[i, METRIC], a0[i, MASK], level)
            return carry

        lax.fori_loop(1, STRIP + 1, strip_row, 0, unroll=True)

    for g in range(GROUPS):
        def merge(i, carry, g=g):
            for f in range(FIELDS):
                strip = a0[i + 1, f]
                new = s4[g * STRIP + i, f]
                new = jnp.where(lane < WIDTH, pltpu.roll(strip, (-16 * g - WIDTH) % COLS, 1), new)
                new = jnp.where(lane >= COLS - WIDTH, pltpu.roll(strip, (52 - 16 * g) % COLS, 1), new)
                out[pl.ds(f * LEV * ROWS + g * STRIP + i - WIDTH, LEV, stride=ROWS), :] = new
            return carry

        lax.fori_loop(max(0, WIDTH - g * STRIP), min(STRIP, WIDTH + ROWS - g * STRIP), merge, 0, unroll=True)
    arrived(s0.at[pl.ds(0, pieces * part * HALF // (FIELDS + 2))], out_s)
    for wait in sent:
        wait()


def solution(mesh):
    members, nx, ny = (mesh.shape[axis] for axis in ("member", "dx", "dy"))
    chips = members // 2
    part = (ROWS // 2) // chips
    flat = FIELDS * LEV * ROWS

    def on_device(states, control, owner, map_factor, terrain):
        any_space = pl.BlockSpec(memory_space=pl.ANY)
        dma = pltpu.SemaphoreType.DMA
        out = pl.pallas_call(
            functools.partial(kernel, members, nx, ny),
            out_shape=pltpu.VMEM((flat, COLS), F32),
            in_specs=[any_space] * 5,
            out_specs=pl.BlockSpec(memory_space=pltpu.VMEM),
            scratch_shapes=[
                pltpu.VMEM((flat, COLS), F32),
                pltpu.VMEM((flat, COLS), F32),
                pltpu.SMEM((members,), jnp.int32),
                pltpu.VMEM((ROWS, COLS), F32),
                pltpu.VMEM((ROWS, COLS), jnp.int32),
                pltpu.VMEM((TALL, FIELDS + 2) + TILE, F32),
                pltpu.VMEM((TALL, FIELDS) + TILE, F32),
                pltpu.VMEM((TALL, FIELDS) + TILE, F32),
                pltpu.VMEM((TALL, FIELDS) + TILE, F32),
                pltpu.VMEM((TALL, FIELDS) + TILE, F32),
                pltpu.VMEM((ROWS, FIELDS) + TILE, F32),
                pltpu.VMEM((ROWS, HALF) + TILE, F32),
                pltpu.VMEM((ROWS, HALF) + TILE, F32),
                pltpu.VMEM((2, part * (chips - 1), HALF) + TILE, F32),
                pltpu.VMEM((TALL, FIELDS) + TILE, F32),
                pltpu.VMEM((2,) + TILE, F32),
                pltpu.VMEM((2,) + TILE, F32),
                pltpu.VMEM((STRIP + 2, FIELDS + 2) + TILE, F32),
                pltpu.VMEM((STRIP + 2, FIELDS) + TILE, F32),
                pltpu.VMEM((2, FIELDS + 2) + TILE, F32),
                pltpu.VMEM((2, FIELDS + 2) + TILE, F32),
                pltpu.VMEM((2,) + TILE, F32),
                pltpu.VMEM((2,) + TILE, F32),
                dma((5,)),
                dma, dma((chips,)), dma, dma((2,)), dma((chips - 1,)), dma,
                dma, dma,
                dma, dma((chips - 1,)),
                dma((2,)), dma((2,)),
                dma((2,)), dma((2,)),
                dma((2,)), dma((2,)),
                dma((4,)), dma((4,)),
            ],
            compiler_params=pltpu.CompilerParams(collective_id=0, has_side_effects=True),
        )(states.reshape(flat, COLS), control.reshape(flat, COLS), owner, map_factor, terrain)
        return out.reshape(states.shape)

    spread = P("member", None, None, "dx", "dy")
    return jax.shard_map(
        on_device,
        mesh=mesh,
        in_specs=(spread, spread, P(), P("dx", "dy"), P("dx", "dy")),
        out_specs=spread,
        check_vma=False,
    )
```

time: 45.8 us -> 40.9 us (0.89)
  the two profiles are of different devices: /device:TPU:15 before, /device:TPU:14 now
where the time goes in v2:
time: 40.9 us; the launch traced here: 40.8 us
  Pallas kernels  40 us (98%)
  local copies, waits for them, and re-layouts  0.71 us (2%)
    pallas_call x1, Pallas kernels, on_device(): pl.pallas_call(functools.partial(kernel, members, nx, ny), out_shape=pltp...  40 us

profile of v2, /device:TPU:14, one launch (start us, length us, event | category | flops | bytes accessed | tf_op | source)
XLA Modules:
  0.0 40.8 jit_solution(4639825099570131175)
XLA Ops:
  0.0 40.0 %shard_map.55 = f32[512,128]{1,0:T(8,128)S(1)} custom-call(f32[512,128]{1,0:T(8,128)} %bitcast.4, f32[512,128]{1,0:T(8,128)} %bitcast.5, s32[16]{0:T(128)} %owner_hbm.1, f32[16,128]{1,0:T(8,128)} %map_hbm.1, s32[16,128]{1,0:T(8,128)} %ter_hbm.1), custom_call_target="tpu_custom_call" | custom-call | tf_op jit(solution)/shard_map/pallas_call | solution.py:480
  40.1 0.7 %copy.7 = f32[1,4,8,16,128]{4,3,2,1,0:T(8,128)} copy(f32[1,4,8,16,128]{4,3,2,1,0:T(8,128)S(1)} %bitcast.3) | data formatting | bytes 524288

commit v3 on v2

--- a/solution.py
+++ b/solution.py
@@ -55,9 +55,9 @@
 def kernel(
     members, nx, ny,
     p_hbm, c_hbm, owner_hbm, map_hbm, ter_hbm, out,
-    pv, cv, owner, mv, tv, s0, s1, s2, s3, s4, q, qr, t, rr, dx_rows, mts, mtr, a0, a1, es, er, hs, hr,
+    pv, cv, owner, mv, tv, s0, s1, s2, s3, s4, q, qr, t, rr, dx_rows, mts, mtr, a0, a1, es, er, pcs, pcr, dcs, crr, crm, cs,
     local_sem, out_s, dd_r, dm_r, rs_r, ag_r, fw_r, hx_s, hx_r, ha_s, ha_r, hf_s, hf_r,
-    ph_s, ph_r, mt_s, mt_r, ed_s, ed_r,
+    ph_s, ph_r, mt_s, mt_r, ed_s, ed_r, pc_s, pc_r, dc_s, dc_r, cs_s, cs_r,
 ):
     chips = members // 2
     part = (ROWS // 2) // chips
@@ -130,6 +130,12 @@
     greet(partner)
     pl.when(has_s)(lambda: greet({"dy": y - 1}))
     pl.when(has_n)(lambda: greet({"dy": y + 1}))
+    corners = [(e, w) for e in range(2) for w in range(2)]
+    to_corner = {(e, w): {"dx": x + (1, -1)[w], "dy": y + (1, -1)[e]} for e, w in corners}
+    gives_corner = {(e, w): jnp.logical_and((has_e, has_w)[w], (has_n, has_s)[e]) for e, w in corners}
+    takes_corner = {(e, w): jnp.logical_and((has_w, has_e)[w], (has_s, has_n)[e]) for e, w in corners}
+    for key in corners:
+        pl.when(gives_corner[key])(lambda key=key: greet(to_corner[key]))
 
     level = lax.broadcasted_iota(jnp.int32, TILE, 0)
     lane = lax.broadcasted_iota(jnp.int32, TILE, 1)
@@ -155,7 +161,7 @@
     lax.fori_loop(ROWS - WIDTH, ROWS, first, 0, unroll=2)
     pl.semaphore_wait(
         barrier,
-        chips + has_w.astype(jnp.int32) + has_e.astype(jnp.int32) + has_s.astype(jnp.int32) + has_n.astype(jnp.int32),
+        chips + sum(there.astype(jnp.int32) for there in (has_w, has_e, has_s, has_n, *takes_corner.values())),
     )
 
     def dd(kind, d):
@@ -208,6 +214,27 @@
         pl.when(there)(lambda side=side: mt_halo(side).start())
         sent.append(lambda side=side, there=there: pl.when(there)(mt_halo(side).wait_send))
 
+    quad = lax.div(lane, WIDTH)
+
+    def p_corner(e, w):
+        return remote(pcs.at[e, w], pcr.at[e, w], pc_s.at[e, w], pc_r.at[e, w], to_corner[e, w])
+
+    for e, w in corners:
+        packed = zero
+        for f in range(FIELDS):
+            for k in range(WIDTH):
+                place = f * 2 * WIDTH + w * WIDTH + k
+                row = s0[(ROWS, WIDTH)[w] + k, f]
+                packed = jnp.where(quad == place, pltpu.roll(row, (place + 1 - e) * WIDTH % COLS, 1), packed)
+        pcs[e, w] = packed
+        pl.when(gives_corner[e, w])(lambda e=e, w=w: p_corner(e, w).start())
+        sent.append(lambda e=e, w=w: pl.when(gives_corner[e, w])(p_corner(e, w).wait_send))
+
+        def no_corner(e=e, w=w):
+            pcr[e, w] = zero
+
+        pl.when(jnp.logical_not(takes_corner[e, w]))(no_corner)
+
     def factors(r, carry):
         s0[r + WIDTH, METRIC] = jnp.broadcast_to(mv[pl.ds(r, 1), :] * (-0.5 * integration_step), TILE)
         ground = jnp.broadcast_to(tv[pl.ds(r, 1), :], TILE)
@@ -224,6 +251,8 @@
                     dx_rows[b0 + b, f] = zero
             mtr[side, pl.ds(0, WIDTH), :] = jnp.ones((WIDTH, COLS), F32)
             mtr[side, pl.ds(WIDTH, WIDTH), :] = jnp.full((WIDTH, COLS), F32(2 * LEV))
+            for n in range(chips):
+                cs[side * chips + n] = zero
         return body
 
     pl.when(jnp.logical_not(has_w))(empty(0, 1))
@@ -233,7 +262,7 @@
         def body():
             for f in range(FIELDS + 2):
                 er[side, f] = zero
-            hr[side] = zero
+            crr[side] = zero
         return body
 
     pl.when(jnp.logical_not(has_s))(no_edge(0))
@@ -265,6 +294,14 @@
     def hf(d):
         rows = pl.ds(halo_b(source(d)), part)
         return remote(dx_rows.at[rows, mine], dx_rows.at[rows, mine], hf_s.at[top(source(d))], hf_r.at[top(source(d))], partner)
+
+    def d_corner(e):
+        return remote(dcs.at[e], crr.at[e], dc_s.at[e], dc_r.at[e], {"dx": at, "dy": y + (1, -1)[e]})
+
+    def cc(member):
+        return remote(crm, cs.at[me], cs_s, cs_r.at[top(chip)], {"member": member})
+
+    own_cc = pltpu.make_async_copy(crm, cs.at[me], cs_r.at[top(chip)])
 
     for kind in range(2):
         b = own_b(kind, chip)
@@ -279,11 +316,33 @@
                 dx_rows[b + n, HALF * core + f] = total[n][f]
         if kind == 0:
             pl.when(gives)(hx.start)
+            north, south = zero, zero
+            for n in range(part):
+                for f in range(HALF):
+                    place = (HALF * core + f) * 2 * WIDTH + chip * part + n + WIDTH - 2 * WIDTH * top(chip)
+                    other = lax.rem(place + 16, 32)
+                    north = jnp.where(quad == place, pltpu.roll(total[n][f], lax.rem(place + 1, 32) * WIDTH, 1), north)
+                    south = jnp.where(quad == other, pltpu.roll(total[n][f], other * WIDTH, 1), south)
+            dcs[0] = north
+            dcs[1] = south
+            for e, there in ((0, has_n), (1, has_s)):
+                going = jnp.logical_and(gives, there)
+                pl.when(going)(lambda e=e: d_corner(e).start())
+                sent.append(lambda e=e, going=going: pl.when(going)(d_corner(e).wait_send))
             sent.append(lambda: pl.when(gives)(hx.wait_send))
         for d in far_first:
             ag(kind, d).start()
         fw(kind, 0).start()
 
+    def spread_halo():
+        hx.wait_recv()
+        for d in far_first:
+            ha(d).start()
+        hf(0).start()
+
+    pl.when(takes)(spread_halo)
+
+    sent.append(lambda: pl.when(takes)(lambda: arrived(rr.at[0], ha_s)))
     def gather(ds):
         for d in ds:
             arrived(dx_rows.at[pl.ds(0, 2 * part), mine], ag_r.at[d - 1])
@@ -291,15 +350,19 @@
                 fw(kind, d).start()
 
     gather(near_first[: chips // 2])
-    def spread_halo():
-        hx.wait_recv()
+
+    def spread_corner():
+        for e, there in ((0, has_s), (1, has_n)):
+            pl.when(there)(lambda e=e: d_corner(e).wait_recv())
+        crm[...] = crr[0] + crr[1]
+        own_cc.start()
         for d in far_first:
-            ha(d).start()
-        hf(0).start()
-
-    pl.when(takes)(spread_halo)
-
-    sent.append(lambda: pl.when(takes)(lambda: arrived(rr.at[0], ha_s)))
+            for co in range(2):
+                cc(2 * peer(d) + co).start()
+        cc(me + 1 - 2 * core).start()
+
+    pl.when(takes)(spread_corner)
+    sent.append(lambda: pl.when(takes)(lambda: arrived(cs.at[pl.ds(0, members - 1)], cs_s)))
     gather(near_first[chips // 2 :])
     arrived(dx_rows.at[pl.ds(0, ROWS), mine], fw_r)
 
@@ -401,23 +464,6 @@
     lax.fori_loop(WIDTH + ROWS, TALL, begin, 0, unroll=2)
 
     lax.fori_loop(0, FIELDS, pack_rows(outside, True), 0)
-    north, south = zero, zero
-    for f in range(FIELDS):
-        for n, b in enumerate(outside):
-            at_lane = f * 32 + n * WIDTH
-            slot = lax.div(lane, WIDTH) == at_lane // WIDTH
-            row = s0[b, f]
-            north = jnp.where(slot, pltpu.roll(row, (at_lane + WIDTH) % COLS, 1), north)
-            south = jnp.where(slot, pltpu.roll(row, at_lane, 1), south)
-    hs[0] = north
-    hs[1] = south
-
-    def corner(side):
-        return remote(hs.at[side], hr.at[side], ed_s.at[2 + side], ed_r.at[2 + side], {"dy": y + (1, -1)[side]})
-
-    for side, there in ((0, has_n), (1, has_s)):
-        pl.when(there)(lambda side=side: corner(side).start())
-        sent.append(lambda side=side, there=there: pl.when(there)(corner(side).wait_send))
 
     for step in range(1, STEPS + 1):
         def rows(j, carry, src=states[step - 1], dst=states[step], step=step):
@@ -427,9 +473,14 @@
 
         lax.fori_loop(0, WIDTH, rows, 0, unroll=True)
 
-    pl.when(has_s)(lambda: corner(0).wait_recv())
-    pl.when(has_n)(lambda: corner(1).wait_recv())
-    from_south, from_north = hr[0], hr[1]
+    for e, w in corners:
+        pl.when(takes_corner[e, w])(lambda e=e, w=w: p_corner(e, w).wait_recv())
+    for side, there in ((0, has_e), (1, has_w)):
+        pl.when(there)(lambda side=side: arrived(cs.at[pl.ds(side * chips, chips)], cs_r.at[side]))
+    by_core = [functools.reduce(jnp.add, [cs[2 * ch + co] for ch in range(chips)]) for co in range(2)]
+    low = lane < COLS // 2
+    from_south = jnp.where(low, by_core[0], by_core[1]) + (pcr[0, 0] + pcr[0, 1])
+    from_north = pltpu.roll(jnp.where(low, by_core[1], by_core[0]), COLS // 2, 1) + (pcr[1, 0] + pcr[1, 1])
     for n, b in enumerate(outside):
         g, i = divmod(b, STRIP)
         left = jnp.logical_and(block == g, inner < WIDTH)
@@ -504,8 +555,12 @@
                 pltpu.VMEM((STRIP + 2, FIELDS) + TILE, F32),
                 pltpu.VMEM((2, FIELDS + 2) + TILE, F32),
                 pltpu.VMEM((2, FIELDS + 2) + TILE, F32),
+                pltpu.VMEM((2, 2) + TILE, F32),
+                pltpu.VMEM((2, 2) + TILE, F32),
                 pltpu.VMEM((2,) + TILE, F32),
                 pltpu.VMEM((2,) + TILE, F32),
+                pltpu.VMEM(TILE, F32),
+                pltpu.VMEM((members,) + TILE, F32),
                 dma((5,)),
                 dma, dma((chips,)), dma, dma((2,)), dma((chips - 1,)), dma,
                 dma, dma,
@@ -513,7 +568,10 @@
                 dma((2,)), dma((2,)),
                 dma((2,)), dma((2,)),
                 dma((2,)), dma((2,)),
-                dma((4,)), dma((4,)),
+                dma((2,)), dma((2,)),
+                dma((2, 2)), dma((2, 2)),
+                dma((2,)), dma((2,)),
+                dma, dma((2,)),
             ],
             compiler_params=pltpu.CompilerParams(collective_id=0, has_side_effects=True),
         )(states.reshape(flat, COLS), control.reshape(flat, COLS), owner, map_factor, terrain)

time: 40.9 us -> 38.7 us (0.946)
  the two profiles are of different devices: /device:TPU:14 before, /device:TPU:15 now
where the time goes in v3:
time: 38.7 us; the launch traced here: 38.2 us
  Pallas kernels  37.5 us (97%)
  local copies, waits for them, and re-layouts  0.71 us (2%)
    pallas_call x1, Pallas kernels, on_device(): pl.pallas_call(functools.partial(kernel, members, nx, ny), out_shape=pltp...  37.5 us

profile of v3, /device:TPU:15, one launch (start us, length us, event | category | flops | bytes accessed | tf_op | source)
XLA Modules:
  0.0 38.2 jit_solution(6605603353955871983)
XLA Ops:
  0.0 37.5 %shard_map.55 = f32[512,128]{1,0:T(8,128)S(1)} custom-call(f32[512,128]{1,0:T(8,128)} %bitcast.4, f32[512,128]{1,0:T(8,128)} %bitcast.5, s32[16]{0:T(128)} %owner_hbm.1, f32[16,128]{1,0:T(8,128)} %map_hbm.1, s32[16,128]{1,0:T(8,128)} %ter_hbm.1), custom_call_target="tpu_custom_call" | custom-call | tf_op jit(solution)/shard_map/pallas_call | solution.py:531
  37.5 0.7 %copy.7 = f32[1,4,8,16,128]{4,3,2,1,0:T(8,128)} copy(f32[1,4,8,16,128]{4,3,2,1,0:T(8,128)S(1)} %bitcast.3) | data formatting | bytes 524288

commit v4 on v3

--- a/solution.py
+++ b/solution.py
@@ -72,6 +72,7 @@
     far_first = sorted(range(1, chips), key=lambda d: -min(d, chips - d))
     near_first = far_first[::-1]
     order = far_first + [0]
+    direct = [d for d in far_first if min(d, chips - d) > 2]
     mine = pl.ds(HALF * core, HALF)
     theirs = pl.ds(HALF * (1 - core), HALF)
     sent = []
@@ -291,9 +292,13 @@
             dx_rows.at[halo_here, mine], dx_rows.at[halo_here, mine], ha_s, ha_r.at[d - 1], same_core(d)
         )
 
+    def both(d):
+        rows = dx_rows.at[halo_here, mine]
+        return remote(rows, rows, ha_s, hf_r.at[top(chip)], {"member": 2 * peer(d) + 1 - core})
+
     def hf(d):
         rows = pl.ds(halo_b(source(d)), part)
-        return remote(dx_rows.at[rows, mine], dx_rows.at[rows, mine], hf_s.at[top(source(d))], hf_r.at[top(source(d))], partner)
+        return remote(dx_rows.at[rows, mine], dx_rows.at[rows, mine], hf_s.at[d], hf_r.at[top(source(d))], partner)
 
     def d_corner(e):
         return remote(dcs.at[e], crr.at[e], dc_s.at[e], dc_r.at[e], {"dx": at, "dy": y + (1, -1)[e]})
@@ -334,55 +339,6 @@
             ag(kind, d).start()
         fw(kind, 0).start()
 
-    def spread_halo():
-        hx.wait_recv()
-        for d in far_first:
-            ha(d).start()
-        hf(0).start()
-
-    pl.when(takes)(spread_halo)
-
-    sent.append(lambda: pl.when(takes)(lambda: arrived(rr.at[0], ha_s)))
-    def gather(ds):
-        for d in ds:
-            arrived(dx_rows.at[pl.ds(0, 2 * part), mine], ag_r.at[d - 1])
-            for kind in range(2):
-                fw(kind, d).start()
-
-    gather(near_first[: chips // 2])
-
-    def spread_corner():
-        for e, there in ((0, has_s), (1, has_n)):
-            pl.when(there)(lambda e=e: d_corner(e).wait_recv())
-        crm[...] = crr[0] + crr[1]
-        own_cc.start()
-        for d in far_first:
-            for co in range(2):
-                cc(2 * peer(d) + co).start()
-        cc(me + 1 - 2 * core).start()
-
-    pl.when(takes)(spread_corner)
-    sent.append(lambda: pl.when(takes)(lambda: arrived(cs.at[pl.ds(0, members - 1)], cs_s)))
-    gather(near_first[chips // 2 :])
-    arrived(dx_rows.at[pl.ds(0, ROWS), mine], fw_r)
-
-    pl.when(has_w)(lambda: p_halo(0).wait_send())
-    pl.when(has_e)(lambda: p_halo(1).wait_send())
-
-    def begin(b, carry):
-        for f in range(FIELDS):
-            s0[b, f] = s0[b, f] + dx_rows[b, f]
-        return carry
-
-    lax.fori_loop(WIDTH, WIDTH + ROWS, begin, 0, unroll=2)
-    states = (s0, s1, s2, s3, s4)
-    for step in range(1, STEPS + 1):
-        def row(b, carry, src=states[step - 1], dst=states[step]):
-            stencil(src, dst, b, s0[b, METRIC], s0[b, MASK], level)
-            return carry
-
-        lax.fori_loop(WIDTH + step, WIDTH + ROWS - step, row, 0, unroll=True)
-
     inner = lax.rem(lane, 16)
     block = lax.div(lane, 16)
 
@@ -405,7 +361,6 @@
 
     inside = range(WIDTH, WIDTH + ROWS)
     outside = [b for b in range(TALL) if b not in inside]
-    lax.fori_loop(0, FIELDS + 2, pack_rows(inside, False), 0)
 
     def halo_factors(side, b0):
         for b in range(WIDTH):
@@ -417,34 +372,94 @@
     pl.when(has_w)(lambda: mt_halo(1).wait_recv())
     halo_factors(0, WIDTH + ROWS)
     halo_factors(1, 0)
-    lax.fori_loop(FIELDS, FIELDS + 2, pack_rows(outside, True), 0)
-
-    for f in range(FIELDS + 2):
-        north, south = zero, zero
-        for i in range(STRIP):
-            strip = a0[i + 1, f]
-            at_lane = (i // 4) * 64 + (i % 4) * 4
-            slot = jnp.logical_and(lax.div(lane, 64) == i // 4, lax.div(inner, 4) == i % 4)
-            north = jnp.where(slot, pltpu.roll(strip, (at_lane - 72) % COLS, 1), north)
-            south = jnp.where(slot, pltpu.roll(strip, (at_lane - 4) % COLS, 1), south)
-        es[0, f] = north
-        es[1, f] = south
-
-    def edge(side):
-        return remote(es.at[side], er.at[side], ed_s.at[side], ed_r.at[side], {"dy": y + (1, -1)[side]})
-
-    for side, there in ((0, has_n), (1, has_s)):
-        pl.when(there)(lambda side=side: edge(side).start())
-        sent.append(lambda side=side, there=there: pl.when(there)(edge(side).wait_send))
+    lax.fori_loop(FIELDS, FIELDS + 2, pack_rows(range(TALL), False), 0, unroll=True)
+
+    def edge(side, late):
+        fields = pl.ds(0, FIELDS) if late else pl.ds(FIELDS, 2)
+        k = side + 2 * late
+        return remote(es.at[side, fields], er.at[side, fields], ed_s.at[k], ed_r.at[k], {"dy": y + (1, -1)[side]})
+
+    def send_edges(late):
+        for f in range(FIELDS) if late else (METRIC, MASK):
+            north, south = zero, zero
+            for i in range(STRIP):
+                strip = a0[i + 1, f]
+                at_lane = (i // 4) * 64 + (i % 4) * 4
+                slot = jnp.logical_and(lax.div(lane, 64) == i // 4, lax.div(inner, 4) == i % 4)
+                north = jnp.where(slot, pltpu.roll(strip, (at_lane - 72) % COLS, 1), north)
+                south = jnp.where(slot, pltpu.roll(strip, (at_lane - 4) % COLS, 1), south)
+            es[0, f] = north
+            es[1, f] = south
+        for side, there in ((0, has_n), (1, has_s)):
+            pl.when(there)(lambda side=side: edge(side, late).start())
+            sent.append(lambda side=side, there=there: pl.when(there)(edge(side, late).wait_send))
+
+    send_edges(0)
+
+    def spread_halo():
+        hx.wait_recv()
+        for d in far_first:
+            ha(d).start()
+            if d in direct:
+                both(d).start()
+        hf(0).start()
+
+    pl.when(takes)(spread_halo)
+
+    spread_bytes = q.at[pl.ds(0, (chips - 1 + len(direct)) * part * HALF // FIELDS)]
+    sent.append(lambda: pl.when(takes)(lambda: arrived(spread_bytes, ha_s)))
+    def gather(ds):
+        for d in ds:
+            arrived(dx_rows.at[pl.ds(0, 2 * part), mine], ag_r.at[d - 1])
+            for kind in range(2):
+                fw(kind, d).start()
+
+    gather(near_first[: chips // 2])
+
+    def spread_corner():
+        for e, there in ((0, has_s), (1, has_n)):
+            pl.when(there)(lambda e=e: d_corner(e).wait_recv())
+        crm[...] = crr[0] + crr[1]
+        own_cc.start()
+        for d in far_first:
+            for co in range(2):
+                cc(2 * peer(d) + co).start()
+        cc(me + 1 - 2 * core).start()
+
+    pl.when(takes)(spread_corner)
+    sent.append(lambda: pl.when(takes)(lambda: arrived(cs.at[pl.ds(0, members - 1)], cs_s)))
+    gather(near_first[chips // 2 :])
+    arrived(dx_rows.at[pl.ds(0, ROWS), mine], fw_r)
+
+    pl.when(has_w)(lambda: p_halo(0).wait_send())
+    pl.when(has_e)(lambda: p_halo(1).wait_send())
+
+    def begin(b, carry):
+        for f in range(FIELDS):
+            s0[b, f] = s0[b, f] + dx_rows[b, f]
+        return carry
+
+    lax.fori_loop(WIDTH, WIDTH + ROWS, begin, 0, unroll=True)
+    lax.fori_loop(0, FIELDS, pack_rows(inside, False), 0, unroll=True)
+    send_edges(1)
+    states = (s0, s1, s2, s3, s4)
+    for step in range(1, STEPS + 1):
+        def row(b, carry, src=states[step - 1], dst=states[step]):
+            stencil(src, dst, b, s0[b, METRIC], s0[b, MASK], level)
+            return carry
+
+        lax.fori_loop(WIDTH + step, WIDTH + ROWS - step, row, 0, unroll=True)
 
     for d in near_first:
         def pass_on(d=d):
             ha(d).wait_recv()
-            hf(d).start()
+            if d not in direct:
+                hf(d).start()
 
         pl.when(came_from(source(d)))(pass_on)
-    pl.when(has_s)(lambda: edge(0).wait_recv())
-    pl.when(has_n)(lambda: edge(1).wait_recv())
+    for late in range(2):
+        pl.when(has_s)(lambda late=late: edge(0, late).wait_recv())
+        pl.when(has_n)(lambda late=late: edge(1, late).wait_recv())
     for i in range(STRIP):
         at_lane = (i // 4) * 64 + (i % 4) * 4
         left = jnp.logical_and(block < GROUPS, inner < WIDTH)
@@ -454,16 +469,18 @@
             strip = jnp.where(left, pltpu.roll(er[0, f], (-at_lane) % COLS, 1), strip)
             strip = jnp.where(right, pltpu.roll(er[1, f], (76 - at_lane) % COLS, 1), strip)
             a0[i + 1, f] = strip
+    for d in range(chips):
+        if d not in direct:
+            sent.append(lambda d=d: pl.when(came_from(source(d)))(hf(d).wait_send))
     for side, there in ((0, has_e), (1, has_w)):
         rows = dx_rows.at[pl.ds(0, WIDTH), mine]
         pl.when(there)(lambda side=side, rows=rows: arrived(rows, hf_r.at[side]))
-        sent.append(lambda side=side, there=there, rows=rows: pl.when(there)(lambda: arrived(rows, hf_s.at[side])))
     pl.when(has_e)(lambda: p_halo(0).wait_recv())
     pl.when(has_w)(lambda: p_halo(1).wait_recv())
-    lax.fori_loop(0, WIDTH, begin, 0, unroll=2)
-    lax.fori_loop(WIDTH + ROWS, TALL, begin, 0, unroll=2)
-
-    lax.fori_loop(0, FIELDS, pack_rows(outside, True), 0)
+    lax.fori_loop(0, WIDTH, begin, 0, unroll=True)
+    lax.fori_loop(WIDTH + ROWS, TALL, begin, 0, unroll=True)
+
+    lax.fori_loop(0, FIELDS, pack_rows(outside, True), 0, unroll=True)
 
     for step in range(1, STEPS + 1):
         def rows(j, carry, src=states[step - 1], dst=states[step], step=step):
@@ -565,10 +582,10 @@
                 dma, dma((chips,)), dma, dma((2,)), dma((chips - 1,)), dma,
                 dma, dma,
                 dma, dma((chips - 1,)),
+                dma((chips,)), dma((2,)),
                 dma((2,)), dma((2,)),
                 dma((2,)), dma((2,)),
-                dma((2,)), dma((2,)),
-                dma((2,)), dma((2,)),
+                dma((4,)), dma((4,)),
                 dma((2, 2)), dma((2, 2)),
                 dma((2,)), dma((2,)),
                 dma, dma((2,)),

time: 38.7 us -> 37.2 us (0.961)
  Pallas kernels: 37.5 us -> 36.3 us
    pallas_call x1, Pallas kernels: 37.5 us -> 36.3 us  [on_device(): pl.pallas_call(functools.partial(kernel, members, nx, ny), out_shape=pltp...]
where the time goes in v4:
time: 37.2 us; the launch traced here: 37 us
  Pallas kernels  36.3 us (98%)
  local copies, waits for them, and re-layouts  0.71 us (2%)
    pallas_call x1, Pallas kernels, on_device(): pl.pallas_call(functools.partial(kernel, members, nx, ny), out_shape=pltp...  36.3 us

profile of v4, /device:TPU:15, one launch (start us, length us, event | category | flops | bytes accessed | tf_op | source)
XLA Modules:
  0.0 37.0 jit_solution(14333031714152962366)
XLA Ops:
  0.0 36.3 %shard_map.55 = f32[512,128]{1,0:T(8,128)S(1)} custom-call(f32[512,128]{1,0:T(8,128)} %bitcast.4, f32[512,128]{1,0:T(8,128)} %bitcast.5, s32[16]{0:T(128)} %owner_hbm.1, f32[16,128]{1,0:T(8,128)} %map_hbm.1, s32[16,128]{1,0:T(8,128)} %ter_hbm.1), custom_call_target="tpu_custom_call" | custom-call | tf_op jit(solution)/shard_map/pallas_call | solution.py:548
  36.3 0.7 %copy.7 = f32[1,4,8,16,128]{4,3,2,1,0:T(8,128)} copy(f32[1,4,8,16,128]{4,3,2,1,0:T(8,128)S(1)} %bitcast.3) | data formatting | bytes 524288

commit v5 on v4

--- a/solution.py
+++ b/solution.py
@@ -55,9 +55,9 @@
 def kernel(
     members, nx, ny,
     p_hbm, c_hbm, owner_hbm, map_hbm, ter_hbm, out,
-    pv, cv, owner, mv, tv, s0, s1, s2, s3, s4, q, qr, t, rr, dx_rows, mts, mtr, a0, a1, es, er, pcs, pcr, dcs, crr, crm, cs,
+    pv, cv, owner, mv, tv, s0, s1, s2, s3, s4, q, qr, t, rr, dx_rows, mts, mtr, a0, a1, es, er, pcs, pcr, dcs, crr, crm, cs, ph,
     local_sem, out_s, dd_r, dm_r, rs_r, ag_r, fw_r, hx_s, hx_r, ha_s, ha_r, hf_s, hf_r,
-    ph_s, ph_r, mt_s, mt_r, ed_s, ed_r, pc_s, pc_r, dc_s, dc_r, cs_s, cs_r,
+    ph_s, ph_r, mt_s, mt_r, ed_s, ed_r, pc_s, pc_r, dc_s, dc_r, cs_s, cs_r, hello, ready, far, ready_far,
 ):
     chips = members // 2
     part = (ROWS // 2) // chips
@@ -124,19 +124,22 @@
     def greet(device):
         pl.semaphore_signal(barrier, inc=1, device_id=device, device_id_type=MESH)
 
-    pl.when(has_w)(lambda: greet({"dx": x - 1}))
-    pl.when(has_e)(lambda: greet({"dx": x + 1}))
-    for d in far_first:
-        greet(same_core(d))
-    greet(partner)
-    pl.when(has_s)(lambda: greet({"dy": y - 1}))
-    pl.when(has_n)(lambda: greet({"dy": y + 1}))
     corners = [(e, w) for e in range(2) for w in range(2)]
     to_corner = {(e, w): {"dx": x + (1, -1)[w], "dy": y + (1, -1)[e]} for e, w in corners}
     gives_corner = {(e, w): jnp.logical_and((has_e, has_w)[w], (has_n, has_s)[e]) for e, w in corners}
     takes_corner = {(e, w): jnp.logical_and((has_w, has_e)[w], (has_s, has_n)[e]) for e, w in corners}
-    for key in corners:
-        pl.when(gives_corner[key])(lambda key=key: greet(to_corner[key]))
+    second = 2 * chip + 1
+    pl.when(core == 1)(lambda: greet(partner))
+    odd = lax.rem(x, 2) == 1
+    even = jnp.logical_not(odd)
+    across = [(has_w, {"dx": x - 1}), (has_e, {"dx": x + 1})] + [(gives_corner[key], to_corner[key]) for key in corners]
+    number_across = sum(there.astype(jnp.int32) for there, _ in across)
+    for there, device in across:
+        pl.when(jnp.logical_and(even, there))(lambda device=device: greet({"member": second, **device}))
+    for d in far_first:
+        greet({"member": 2 * peer(d) + 1})
+    pl.when(has_s)(lambda: greet({"member": second, "dy": y - 1}))
+    pl.when(has_n)(lambda: greet({"member": second, "dy": y + 1}))
 
     level = lax.broadcasted_iota(jnp.int32, TILE, 0)
     lane = lax.broadcasted_iota(jnp.int32, TILE, 1)
@@ -150,29 +153,37 @@
         value = 2.0 * (members - rank) / (members * (members + 1.0))
         weight = weight + jnp.where(owner[rank] == me, F32(value), F32(0.0))
 
-    def first(r, carry):
+    def first(r, carry, keep=None):
         for f in range(FIELDS):
             state = pv[pl.ds(f * LEV * ROWS + r, LEV, stride=ROWS), :]
             other = cv[pl.ds(f * LEV * ROWS + r, LEV, stride=ROWS), :]
             s0[r + WIDTH, f] = state
+            if keep is not None:
+                ph[r - keep, f] = state
             q[r, f] = weight * other - (1.0 / members) * state
         return carry
 
-    lax.fori_loop(0, WIDTH, first, 0, unroll=2)
-    lax.fori_loop(ROWS - WIDTH, ROWS, first, 0, unroll=2)
-    pl.semaphore_wait(
-        barrier,
-        chips + sum(there.astype(jnp.int32) for there in (has_w, has_e, has_s, has_n, *takes_corner.values())),
-    )
+    lax.fori_loop(0, WIDTH, functools.partial(first, keep=0), 0, unroll=2)
+    lax.fori_loop(ROWS - WIDTH, ROWS, functools.partial(first, keep=ROWS - 2 * WIDTH), 0, unroll=2)
+
+    def tell(sem):
+        pl.semaphore_signal(sem, inc=1, device_id=partner, device_id_type=MESH)
+
+    def first_core():
+        pl.semaphore_wait(barrier, 1)
+        tell(hello)
+
+    pl.when(core == 0)(first_core)
+    pl.when(core == 1)(lambda: pl.semaphore_wait(hello, 1))
 
     def dd(kind, d):
         rows = pl.ds(own_b(kind, peer(d)) - WIDTH, part)
         return remote(q.at[rows, theirs], qr.at[rows], out_s, dd_r.at[d] if kind == 0 else dm_r, partner)
 
     def p_halo(side):
-        src, dst, step = ((WIDTH, WIDTH + ROWS, -1), (ROWS, 0, 1))[side]
+        src, dst, step = ((0, WIDTH + ROWS, -1), (WIDTH, 0, 1))[side]
         return remote(
-            s0.at[pl.ds(src, WIDTH), pl.ds(0, FIELDS)], s0.at[pl.ds(dst, WIDTH), pl.ds(0, FIELDS)],
+            ph.at[pl.ds(src, WIDTH)], s0.at[pl.ds(dst, WIDTH), pl.ds(0, FIELDS)],
             ph_s.at[side], ph_r.at[side], {"dx": x + step},
         )
 
@@ -185,7 +196,7 @@
             out_s, rs_r.at[kind], same_core(d),
         )
 
-    def swap_and_send(kind):
+    def swap(kind):
         if kind == 1:
             arrived(qr.at[pl.ds(WIDTH, ROWS // 2)], dm_r)
         for d in order:
@@ -195,24 +206,42 @@
             for n in range(part):
                 for f in range(HALF):
                     t[b + n, f] = q[b + n, HALF * core + f] + qr[b + n, f]
-            if d:
-                rs(kind, d).start()
 
     for d in order:
         dd(0, d).start()
-    pl.when(has_w)(lambda: p_halo(0).start())
-    pl.when(has_e)(lambda: p_halo(1).start())
     lax.fori_loop(WIDTH, ROWS - WIDTH, first, 0, unroll=2)
     for d in order:
         dd(1, d).start()
-    swap_and_send(0)
-    swap_and_send(1)
+    swap(0)
+    swap(1)
+
+    def second_core():
+        others = has_s.astype(jnp.int32) + has_n.astype(jnp.int32) + odd.astype(jnp.int32) * number_across
+        pl.semaphore_wait(barrier, 2 * (chips - 1) + 2 * others)
+        tell(ready)
+        for there, device in across:
+            def answer(device=device):
+                pl.semaphore_signal(far, inc=1, device_id={"member": second, **device}, device_id_type=MESH)
+
+            pl.when(jnp.logical_and(odd, there))(answer)
+
+    pl.when(core == 1)(second_core)
+    pl.when(core == 0)(lambda: pl.semaphore_wait(ready, 1))
+    for kind in range(2):
+        for d in far_first:
+            rs(kind, d).start()
+    def send_states():
+        pl.when(has_w)(lambda: p_halo(0).start())
+        pl.when(has_e)(lambda: p_halo(1).start())
+
+    pl.when(odd)(send_states)
+    for side, there in ((0, has_w), (1, has_e)):
+        sent.append(lambda side=side, there=there: pl.when(there)(p_halo(side).wait_send))
 
     for side, start in ((0, 0), (1, ROWS - WIDTH)):
         mts[side, pl.ds(0, WIDTH), :] = mv[pl.ds(start, WIDTH), :]
         mts[side, pl.ds(WIDTH, WIDTH), :] = tv[pl.ds(start, WIDTH), :].astype(F32)
     for side, there in ((0, has_w), (1, has_e)):
-        pl.when(there)(lambda side=side: mt_halo(side).start())
         sent.append(lambda side=side, there=there: pl.when(there)(mt_halo(side).wait_send))
 
     quad = lax.div(lane, WIDTH)
@@ -228,13 +257,20 @@
                 row = s0[(ROWS, WIDTH)[w] + k, f]
                 packed = jnp.where(quad == place, pltpu.roll(row, (place + 1 - e) * WIDTH % COLS, 1), packed)
         pcs[e, w] = packed
-        pl.when(gives_corner[e, w])(lambda e=e, w=w: p_corner(e, w).start())
         sent.append(lambda e=e, w=w: pl.when(gives_corner[e, w])(p_corner(e, w).wait_send))
 
         def no_corner(e=e, w=w):
             pcr[e, w] = zero
 
         pl.when(jnp.logical_not(takes_corner[e, w]))(no_corner)
+
+    def send_small():
+        for side, there in ((0, has_w), (1, has_e)):
+            pl.when(there)(lambda side=side: mt_halo(side).start())
+        for e, w in corners:
+            pl.when(gives_corner[e, w])(lambda e=e, w=w: p_corner(e, w).start())
+
+    pl.when(odd)(send_small)
 
     def factors(r, carry):
         s0[r + WIDTH, METRIC] = jnp.broadcast_to(mv[pl.ds(r, 1), :] * (-0.5 * integration_step), TILE)
@@ -302,6 +338,11 @@
 
     def d_corner(e):
         return remote(dcs.at[e], crr.at[e], dc_s.at[e], dc_r.at[e], {"dx": at, "dy": y + (1, -1)[e]})
+
+    def send_sums():
+        hx.start()
+        pl.when(has_n)(lambda: d_corner(0).start())
+        pl.when(has_s)(lambda: d_corner(1).start())
 
     def cc(member):
         return remote(crm, cs.at[me], cs_s, cs_r.at[top(chip)], {"member": member})
@@ -320,7 +361,6 @@
             for f in range(HALF):
                 dx_rows[b + n, HALF * core + f] = total[n][f]
         if kind == 0:
-            pl.when(gives)(hx.start)
             north, south = zero, zero
             for n in range(part):
                 for f in range(HALF):
@@ -330,9 +370,9 @@
                     south = jnp.where(quad == other, pltpu.roll(total[n][f], other * WIDTH, 1), south)
             dcs[0] = north
             dcs[1] = south
+            pl.when(jnp.logical_and(odd, gives))(send_sums)
             for e, there in ((0, has_n), (1, has_s)):
                 going = jnp.logical_and(gives, there)
-                pl.when(going)(lambda e=e: d_corner(e).start())
                 sent.append(lambda e=e, going=going: pl.when(going)(d_corner(e).wait_send))
             sent.append(lambda: pl.when(gives)(hx.wait_send))
         for d in far_first:
@@ -362,18 +402,6 @@
     inside = range(WIDTH, WIDTH + ROWS)
     outside = [b for b in range(TALL) if b not in inside]
 
-    def halo_factors(side, b0):
-        for b in range(WIDTH):
-            s0[b0 + b, METRIC] = jnp.broadcast_to(mtr[side, pl.ds(b, 1), :] * (-0.5 * integration_step), TILE)
-            ground = jnp.broadcast_to(mtr[side, pl.ds(WIDTH + b, 1), :], TILE)
-            s0[b0 + b, MASK] = (level_f >= ground).astype(F32)
-
-    pl.when(has_e)(lambda: mt_halo(0).wait_recv())
-    pl.when(has_w)(lambda: mt_halo(1).wait_recv())
-    halo_factors(0, WIDTH + ROWS)
-    halo_factors(1, 0)
-    lax.fori_loop(FIELDS, FIELDS + 2, pack_rows(range(TALL), False), 0, unroll=True)
-
     def edge(side, late):
         fields = pl.ds(0, FIELDS) if late else pl.ds(FIELDS, 2)
         k = side + 2 * late
@@ -394,6 +422,41 @@
             pl.when(there)(lambda side=side: edge(side, late).start())
             sent.append(lambda side=side, there=there: pl.when(there)(edge(side, late).wait_send))
 
+    def gather(ds):
+        for d in ds:
+            arrived(dx_rows.at[pl.ds(0, 2 * part), mine], ag_r.at[d - 1])
+            for kind in range(2):
+                fw(kind, d).start()
+
+    starts_last = jnp.logical_and(x == 0, y == 0)
+    pl.when(jnp.logical_not(starts_last))(lambda: gather(near_first))
+
+    def all_answered():
+        pl.semaphore_wait(far, number_across)
+        tell(ready_far)
+
+    pl.when(jnp.logical_and(even, core == 1))(all_answered)
+    pl.when(jnp.logical_and(even, core == 0))(lambda: pl.semaphore_wait(ready_far, 1))
+
+    def send_across():
+        pl.when(gives)(send_sums)
+        send_states()
+        send_small()
+
+    pl.when(even)(send_across)
+
+    def halo_factors(side, b0):
+        for b in range(WIDTH):
+            s0[b0 + b, METRIC] = jnp.broadcast_to(mtr[side, pl.ds(b, 1), :] * (-0.5 * integration_step), TILE)
+            ground = jnp.broadcast_to(mtr[side, pl.ds(WIDTH + b, 1), :], TILE)
+            s0[b0 + b, MASK] = (level_f >= ground).astype(F32)
+
+    pl.when(has_e)(lambda: mt_halo(0).wait_recv())
+    pl.when(has_w)(lambda: mt_halo(1).wait_recv())
+    halo_factors(0, WIDTH + ROWS)
+    halo_factors(1, 0)
+    lax.fori_loop(FIELDS, FIELDS + 2, pack_rows(range(TALL), False), 0, unroll=True)
+
     send_edges(0)
 
     def spread_halo():
@@ -408,14 +471,6 @@
 
     spread_bytes = q.at[pl.ds(0, (chips - 1 + len(direct)) * part * HALF // FIELDS)]
     sent.append(lambda: pl.when(takes)(lambda: arrived(spread_bytes, ha_s)))
-    def gather(ds):
-        for d in ds:
-            arrived(dx_rows.at[pl.ds(0, 2 * part), mine], ag_r.at[d - 1])
-            for kind in range(2):
-                fw(kind, d).start()
-
-    gather(near_first[: chips // 2])
-
     def spread_corner():
         for e, there in ((0, has_s), (1, has_n)):
             pl.when(there)(lambda e=e: d_corner(e).wait_recv())
@@ -428,11 +483,9 @@
 
     pl.when(takes)(spread_corner)
     sent.append(lambda: pl.when(takes)(lambda: arrived(cs.at[pl.ds(0, members - 1)], cs_s)))
-    gather(near_first[chips // 2 :])
+    pl.when(starts_last)(lambda: gather(near_first))
     arrived(dx_rows.at[pl.ds(0, ROWS), mine], fw_r)
 
-    pl.when(has_w)(lambda: p_halo(0).wait_send())
-    pl.when(has_e)(lambda: p_halo(1).wait_send())
 
     def begin(b, carry):
         for f in range(FIELDS):
@@ -578,6 +631,7 @@
                 pltpu.VMEM((2,) + TILE, F32),
                 pltpu.VMEM(TILE, F32),
                 pltpu.VMEM((members,) + TILE, F32),
+                pltpu.VMEM((2 * WIDTH, FIELDS) + TILE, F32),
                 dma((5,)),
                 dma, dma((chips,)), dma, dma((2,)), dma((chips - 1,)), dma,
                 dma, dma,
@@ -589,6 +643,7 @@
                 dma((2, 2)), dma((2, 2)),
                 dma((2,)), dma((2,)),
                 dma, dma((2,)),
+                *[pltpu.SemaphoreType.REGULAR] * 4,
             ],
             compiler_params=pltpu.CompilerParams(collective_id=0, has_side_effects=True),
         )(states.reshape(flat, COLS), control.reshape(flat, COLS), owner, map_factor, terrain)

time: 37.2 us -> 36.1 us (0.970)
  Pallas kernels: 36.3 us -> 34.9 us
    pallas_call x1, Pallas kernels: 36.3 us -> 34.9 us  [on_device(): pl.pallas_call(functools.partial(kernel, members, nx, ny), out_shape=pltp...]
where the time goes in v5:
time: 36.1 us; the launch traced here: 35.6 us
  Pallas kernels  34.9 us (97%)
  local copies, waits for them, and re-layouts  0.71 us (2%)
    pallas_call x1, Pallas kernels, on_device(): pl.pallas_call(functools.partial(kernel, members, nx, ny), out_shape=pltp...  34.9 us

profile of v5, /device:TPU:15, one launch (start us, length us, event | category | flops | bytes accessed | tf_op | source)
XLA Modules:
  0.0 35.6 jit_solution(17796722553462595545)
XLA Ops:
  0.0 34.9 %shard_map.55 = f32[512,128]{1,0:T(8,128)S(1)} custom-call(f32[512,128]{1,0:T(8,128)} %bitcast.4, f32[512,128]{1,0:T(8,128)} %bitcast.5, s32[16]{0:T(128)} %owner_hbm.1, f32[16,128]{1,0:T(8,128)} %map_hbm.1, s32[16,128]{1,0:T(8,128)} %ter_hbm.1), custom_call_target="tpu_custom_call" | custom-call | tf_op jit(solution)/shard_map/pallas_call | solution.py:601
  34.9 0.7 %copy.7 = f32[1,4,8,16,128]{4,3,2,1,0:T(8,128)} copy(f32[1,4,8,16,128]{4,3,2,1,0:T(8,128)S(1)} %bitcast.3) | data formatting | bytes 524288

commit v6 on v5

--- a/solution.py
+++ b/solution.py
@@ -72,7 +72,7 @@
     far_first = sorted(range(1, chips), key=lambda d: -min(d, chips - d))
     near_first = far_first[::-1]
     order = far_first + [0]
-    direct = [d for d in far_first if min(d, chips - d) > 2]
+    direct = [d for d in far_first if min(d, chips - d) > 3]
     mine = pl.ds(HALF * core, HALF)
     theirs = pl.ds(HALF * (1 - core), HALF)
     sent = []

time: 36.1 us -> 36.1 us (level)
  no operation moved by 1% of the time
where the time goes in v6:
time: 36.1 us; the launch traced here: 35.6 us
  Pallas kernels  34.9 us (97%)
  local copies, waits for them, and re-layouts  0.71 us (2%)
    pallas_call x1, Pallas kernels, on_device(): pl.pallas_call(functools.partial(kernel, members, nx, ny), out_shape=pltp...  34.9 us

profile of v6, /device:TPU:15, one launch (start us, length us, event | category | flops | bytes accessed | tf_op | source)
XLA Modules:
  0.0 35.6 jit_solution(1464782150700053184)
XLA Ops:
  0.0 34.9 %shard_map.55 = f32[512,128]{1,0:T(8,128)S(1)} custom-call(f32[512,128]{1,0:T(8,128)} %bitcast.4, f32[512,128]{1,0:T(8,128)} %bitcast.5, s32[16]{0:T(128)} %owner_hbm.1, f32[16,128]{1,0:T(8,128)} %map_hbm.1, s32[16,128]{1,0:T(8,128)} %ter_hbm.1), custom_call_target="tpu_custom_call" | custom-call | tf_op jit(solution)/shard_map/pallas_call | solution.py:601
  34.9 0.7 %copy.7 = f32[1,4,8,16,128]{4,3,2,1,0:T(8,128)} copy(f32[1,4,8,16,128]{4,3,2,1,0:T(8,128)S(1)} %bitcast.3) | data formatting | bytes 524288
